TPU v7x, 256 devices: a whole 4x4x8 slice. The times are simulated.
256 devices in a mesh: slab: 16 (over y, x), tile: 4 (over z_lo, core), view: 4 (over z_hi).
Axes of the slice: x: 4, y: 4, z: 8 (z_hi: 4, z_lo: 2; z = z_hi * 2 + z_lo), core: 2. Of those that a mesh axis runs over, the one named last changes fastest.
Arguments:
- estimate: float32 [256, 256, 128], P('slab', 'tile'), may hold values from 0.25 to 4
- measured: float32 [4, 256, 256, 128], P('view', 'slab', 'tile'), may hold values from 0.25 to 4
- psf_taps: float32 [4, 3, 31], P('view'), may hold values from 0.3 to 1
- plane_source: int32 [4, 256], P('view'), may hold values from 0 to 255, as said below
- plane_shift: int32 [4, 256], P('view'), may hold values from 0 to 127
Outputs:
- new_estimate: float32 [256, 256, 128], P('slab', 'tile', 'view')
Inputs may be any that keep to these rules, and one draw needn't show every extreme that they name: `plane_source`: for each view, the 16 camera planes of one aligned block of 16 take their sample planes from 8 different aligned blocks of 16 sample planes, exactly 2 from each; a sample plane may be shown several times or not at all.
All inputs are finite; a program needn't handle non-finite values.
Results may differ from a plain program's by a relative error of at most 0.0001.
Values sent between devices are 32-bit elements; how exact they have to be, the bound alone decides.
A program may use at most 64 MiB of HBM per device.

v0:
```python
import jax
import jax.numpy as jnp
from jax import lax
from jax.sharding import PartitionSpec as P

exact_mode = lax.Precision.HIGHEST


def extended_2(cells, sides, width):
    for axis, dim in sides:
        count = lax.axis_size(axis)
        head = lax.slice_in_dim(cells, 0, width, axis=dim)
        tail = lax.slice_in_dim(cells, cells.shape[dim] - width, cells.shape[dim], axis=dim)
        cells = jnp.concatenate(
            [
                lax.ppermute(tail, axis, [(i, (i + 1) % count) for i in range(count)]),
                cells,
                lax.ppermute(head, axis, [((i + 1) % count, i) for i in range(count)]),
            ],
            axis=dim,
        )
    return cells


def band_matrix(kernel, length, radius):
    shape_band = (length, length + 2 * radius)
    row_index = lax.broadcasted_iota(jnp.int32, shape_band, 0)
    col_index = lax.broadcasted_iota(jnp.int32, shape_band, 1)
    offset = col_index - row_index
    tap_count = kernel.shape[0]
    inside = (offset >= 0) & (offset < tap_count)
    padded = jnp.concatenate([kernel, jnp.zeros((1,), jnp.float32)])
    return jnp.take(padded, jnp.where(inside, offset, tap_count))


def apply_depth(extended, kernel, length, radius):
    band_rows = band_matrix(kernel, length, radius)
    return jnp.einsum("ij,jab->iab", band_rows, extended, precision=exact_mode)


def apply_rows(extended, kernel, length, radius):
    band_rows = band_matrix(kernel, length, radius)
    return jnp.einsum("ij,ajb->aib", band_rows, extended, precision=exact_mode)


def blur_depth_rim(volume, kernel):
    radius = (kernel.shape[0] - 1) // 2
    extended = extended_2(volume, (("slab", 0),), radius)
    return apply_depth(extended, kernel, volume.shape[0], radius)


def blur_rows(volume, kernel):
    radius = (kernel.shape[0] - 1) // 2
    extended = extended_2(volume, (("tile", 1),), radius)
    return apply_rows(extended, kernel, volume.shape[1], radius)


def blur_columns(volume, kernel):
    radius = (kernel.shape[0] - 1) // 2
    x_width = volume.shape[2]
    shape_circ = (x_width, x_width)
    source_index = lax.broadcasted_iota(jnp.int32, shape_circ, 0)
    out_index = lax.broadcasted_iota(jnp.int32, shape_circ, 1)
    offset = jnp.mod(source_index - out_index + radius, x_width)
    tap_count = kernel.shape[0]
    inside = offset < tap_count
    padded = jnp.concatenate([kernel, jnp.zeros((1,), jnp.float32)])
    weights = jnp.take(padded, jnp.where(inside, offset, tap_count))
    return jnp.einsum("abj,ji->abi", volume, weights, precision=exact_mode)


def shear_planes(volume, shifts, direction):
    x_width = volume.shape[2]
    doubled = jnp.concatenate([volume, volume], axis=2)
    starts = jnp.mod(-direction * shifts, x_width)

    def one_plane(pair):
        plane, start = pair
        return lax.dynamic_slice_in_dim(plane, start, x_width, 1)

    return lax.map(one_plane, (doubled, starts))


def routing(sources, planes, devices, capacity, own_index):
    source_table = sources.reshape(devices, planes)
    owners = source_table // planes
    within = source_table % planes
    is_later = lax.broadcasted_iota(jnp.int32, (planes, planes), 0) > lax.broadcasted_iota(
        jnp.int32, (planes, planes), 1
    )
    same_owner = (owners[:, :, None] == owners[:, None, :]) & is_later[None]
    ranks = jnp.sum(same_owner.astype(jnp.int32), axis=2)
    slot_hot = (ranks[:, :, None] == jnp.arange(capacity, dtype=jnp.int32)[None, None, :]).astype(
        jnp.float32
    )
    plane_hot = (within[:, :, None] == jnp.arange(planes, dtype=jnp.int32)[None, None, :]).astype(
        jnp.float32
    )
    from_self = (owners == own_index).astype(jnp.float32)
    selector = jnp.einsum("cj,cjk,cjl->ckl", from_self, slot_hot, plane_hot, precision=exact_mode)
    own_owners = lax.dynamic_index_in_dim(owners, own_index, 0, keepdims=False)
    own_slots = lax.dynamic_index_in_dim(slot_hot, own_index, 0, keepdims=False)
    source_hot = (own_owners[:, None] == jnp.arange(devices, dtype=jnp.int32)[None, :]).astype(
        jnp.float32
    )
    picker = (source_hot[:, :, None] * own_slots[:, None, :]).reshape(planes, devices * capacity)
    return (selector, picker)


def route_planes(buffer):
    return lax.all_to_all(buffer, "slab", split_axis=0, concat_axis=0, tiled=True)


def local(estimate, measured, psf_taps, plane_source, plane_shift):
    kernels = psf_taps[0] / jnp.sum(psf_taps[0], axis=1, keepdims=True)
    flipped = kernels[:, ::-1]
    planes, rows_dev, x_width = estimate.shape
    devices = lax.axis_size("slab")
    capacity = max(2, planes // devices)
    own_index = lax.axis_index("slab")
    sources = plane_source[0]
    own_shifts = lax.dynamic_slice_in_dim(plane_shift[0], own_index * planes, planes)
    blurred = blur_columns(blur_rows(blur_depth_rim(estimate, kernels[0]), kernels[1]), kernels[2])
    selector, picker = routing(sources, planes, devices, capacity, own_index)
    outgoing = jnp.einsum("ckl,lab->ckab", selector, blurred, precision=exact_mode)
    incoming = route_planes(outgoing)
    camera = jnp.einsum(
        "jm,mab->jab",
        picker,
        incoming.reshape(devices * capacity, rows_dev, x_width),
        precision=exact_mode,
    )
    forward = shear_planes(camera, own_shifts, 1)
    ratio_planes = measured[0] / forward
    unsheared = shear_planes(ratio_planes, own_shifts, -1)
    returning = jnp.einsum("jm,jab->mab", picker, unsheared, precision=exact_mode)
    arrived = route_planes(returning.reshape(devices, capacity, rows_dev, x_width))
    pulled = jnp.einsum("ckl,ckab->lab", selector, arrived, precision=exact_mode)
    correction = blur_depth_rim(blur_rows(blur_columns(pulled, flipped[2]), flipped[1]), flipped[0])
    view_count = lax.axis_size("view")
    share_width = x_width // view_count
    start_col = lax.axis_index("view") * share_width
    own_part = lax.dynamic_slice_in_dim(estimate, start_col, share_width, 2)
    summed = lax.dynamic_slice_in_dim(lax.psum(correction, "view"), start_col, share_width, 2)
    return own_part * summed / view_count


def solution(mesh):
    in_specs = (
        P("slab", "tile", None),
        P("view", "slab", "tile", None),
        P("view", None, None),
        P("view", None),
        P("view", None),
    )
    out_specs = P("slab", "tile", "view")
    return jax.shard_map(local, mesh=mesh, in_specs=in_specs, out_specs=out_specs, check_vma=False)
```

profile of v0, /device:TPU:1, one launch (start us, length us, event | category | flops | bytes accessed | tf_op | source)
XLA Modules:
  0.0 509.8 jit_solution(12057729650246626905)
XLA Ops:
  6.5 1.4 copy.36
  8.0 2.1 collective-permute-start
  10.1 3.8 collective-permute-start.1
  14.5 4.8 gather_fusion.1
  19.7 33.9 %gather_fusion.2 = f32[6016]{0:T(1024)S(1)} fusion(f32[32]{0:T(128)S(1)} %get-tuple-element.189, s32[6144]{0:T(1024)S(1)} %pad_clamp_fusion), kind=kCustom, calls=%fused_computation.1.clone | custom fusion | bytes 72192 | tf_op jit(solution)/shard_map/jit(_take)/gather | solution.py:33
  55.0 97.2 %gather_fusion.3 = f32[16384]{0:T(1024)S(1)} fusion(f32[32]{0:T(128)S(1)} %pad_maximum_fusion.6, s32[16384]{0:T(1024)S(1)} %bitcast_clamp_fusion), kind=kCustom, calls=%fused_computation.2.clone | custom fusion | bytes 196608 | tf_op jit(solution)/shard_map/jit(_take)/gather | solution.py:68
  152.7 2.1 fusion
  154.8 2.6 collective-permute-start.2
  158.0 1.3 collective-permute-done.2
  159.3 3.3 collective-permute-done.3
  162.6 0.9 convolution_bitcast_fusion.2
  163.5 0.8 convolution_bitcast_fusion.1
  164.4 1.0 fusion.35
  165.3 1.3 copy.43
  166.6 4.0 all-to-all-start
  170.9 17.1 %all-to-all-done = f32[16,2,64,128]{3,2,1,0:T(8,128)S(1)} async-done(((f32[16,2,64,128]{3,2,1,0:T(8,128)}), f32[16,2,64,128]{3,2,1,0:T(8,128)S(1)}, u32[]{:S(2)}, u32[]{:S(2)}) %all-to-all-start) | async-done | bytes 1048608 | tf_op jit(solution)/shard_map/all_to_all | solution.py:111
  187.9 1.2 convolution_bitcast_fusion.4
  189.2 46.9 %while.26 = (s32[]{:T(128)}, f32[16,64,128]{2,1,0:T(8,128)S(1)}, s32[16]{0:T(128)S(1)}, f32[16,64,256]{2,0,1:T(8,128)S(1)}, s32[]{:T(128)}, /*index=5*/s32[]{:T(128)}, s32[]{:T(128)}, s32[]{:T(128)}, s32[]{:T(128)}) while((s32[]{:T(128)}, f32[16,64,128]{2,1,0:T(8,128)S(1)}, s32[16]{0:T(128)S(1)}, f32[16,64,256]{2,0,1:T(8,128)S(1)}, s32[]{:T(128)}, ...), condition=%wide.region_3.7_spmd, body=%wide.region_2.6_spmd.sunk | while | flops 7 | bytes 131255 | solution.py:81
  189.2 0.7 dynamic_slice.79
  192.1 0.7 dynamic_slice.79
  195.1 0.7 dynamic_slice.79
  198.0 0.7 dynamic_slice.79
  200.9 0.7 dynamic_slice.79
  203.9 0.7 dynamic_slice.79
  206.8 0.7 dynamic_slice.79
  209.7 0.7 dynamic_slice.79
  212.7 0.7 dynamic_slice.79
  215.6 0.7 dynamic_slice.79
  218.5 0.7 dynamic_slice.79
  221.5 0.7 dynamic_slice.79
  224.4 0.7 dynamic_slice.79
  227.3 0.7 dynamic_slice.79
  230.3 0.7 dynamic_slice.79
  233.2 0.7 dynamic_slice.79
  236.3 47.9 %while.27 = (s32[]{:T(128)}, f32[16,64,128]{2,0,1:T(8,128)S(1)}, s32[16]{0:T(128)S(1)}, f32[16,64,256]{2,1,0:T(8,128)S(1)}, s32[]{:T(128)}, /*index=5*/s32[]{:T(128)}, s32[]{:T(128)}, s32[]{:T(128)}, s32[]{:T(128)}) while((s32[]{:T(128)}, f32[16,64,128]{2,0,1:T(8,128)S(1)}, s32[16]{0:T(128)S(1)}, f32[16,64,256]{2,1,0:T(8,128)S(1)}, s32[]{:T(128)}, ...), condition=%wide.region_5.9_spmd, body=%wide.region_4.8_spmd.sunk | while | flops 7 | bytes 131255 | solution.py:81
  236.3 0.7 dynamic_slice.82
  239.3 0.7 dynamic_slice.82
  242.3 0.7 dynamic_slice.82
  245.3 0.7 dynamic_slice.82
  248.3 0.7 dynamic_slice.82
  251.3 0.7 dynamic_slice.82
  254.3 0.7 dynamic_slice.82
  257.3 0.7 dynamic_slice.82
  260.3 0.7 dynamic_slice.82
  263.2 0.7 dynamic_slice.82
  266.2 0.7 dynamic_slice.82
  269.2 0.7 dynamic_slice.82
  284.2 1.0 fusion.16
  285.1 1.3 copy.49
  286.4 3.7 all-to-all-start.1
  290.5 97.2 %gather_fusion.4 = f32[16384]{0:T(1024)S(1)} fusion(f32[32]{0:T(128)S(1)} %pad_maximum_fusion.5, s32[16384]{0:T(1024)S(1)} %bitcast_clamp_fusion), kind=kCustom, calls=%fused_computation.5.clone | custom fusion | bytes 196608 | tf_op jit(solution)/shard_map/jit(_take)/gather | solution.py:68
  387.7 1.2 convolution_bitcast_fusion.3
  388.9 0.7 fusion.19
  389.6 3.6 collective-permute-start.4
  393.2 33.9 %gather_fusion.5 = f32[6016]{0:T(1024)S(1)} fusion(f32[32]{0:T(128)S(1)} %get-tuple-element.188, s32[6144]{0:T(1024)S(1)} %pad_clamp_fusion), kind=kCustom, calls=%fused_computation.4.clone | custom fusion | bytes 72192 | tf_op jit(solution)/shard_map/jit(_take)/gather | solution.py:33
  427.3 0.8 convolution_bitcast_fusion
  428.2 1.6 collective-permute-start.6
  429.8 3.7 collective-permute-start.7
  433.5 4.8 gather_fusion
  438.4 6.3 %collective-permute-done.6 = f32[15,64,128]{2,1,0:T(8,128)S(1)} collective-permute-done((f32[15,64,128]{2,1,0:T(8,128)S(1)}, f32[15,64,128]{2,1,0:T(8,128)S(1)}, u32[]{:S(2)}, u32[]{:S(2)}) %collective-permute-start.6) | collective-permute-done | bytes 491552 | tf_op jit(solution)/shard_map/ppermute | solution.py:16
  444.8 2.5 fusion.6
  447.3 53.3 %all-reduce.2.cloned.1.call-done = f32[16,64,128]{2,0,1:T(8,128)} async-done(((f32[16,64,128]{2,0,1:T(8,128)}), f32[16,64,128]{2,0,1:T(8,128)}) %all-reduce.2.cloned.1.call-update) | async-done | bytes 524304 | tf_op jit(solution)/shard_map/psum | solution.py:144
  500.6 1.4 multiply_multiply_fusion
  502.0 0.9 copy.54
  (133 shorter events, 13.3 us)
Async XLA Ops:
  6.5 7.5 %copy-start.1 = (f32[1,3,31]{2,0,1:T(1,128)S(1)}, f32[1,3,31]{2,0,1:T(1,128)}, u32[]{:S(2)}) copy-start(f32[1,3,31]{2,0,1:T(1,128)} %param.17) | copy-start | bytes 1120
  8.0 144.7 %collective-permute-start = (f32[15,64,128]{2,0,1:T(8,128)S(1)}, f32[15,64,128]{2,0,1:T(8,128)S(1)}, u32[]{:S(2)}, u32[]{:S(2)}) collective-permute-start(f32[15,64,128]{2,0,1:T(8,128)S(1)} %get-tuple-element.176), channel_id=1, source_target_pairs={{0,16},{16,32},{32,48},{48,64},{64,80},{80,96},{96,112},{112,128},... | collective-permute-start | bytes 1474568 | tf_op jit(solution)/shard_map/ppermute | solution.py:16
  10.1 142.6 %collective-permute-start.1 = (f32[15,64,128]{2,0,1:T(8,128)S(1)}, f32[15,64,128]{2,0,1:T(8,128)}, u32[]{:S(2)}, u32[]{:S(2)}) collective-permute-start(f32[15,64,128]{2,0,1:T(8,128)S(1)} %get-tuple-element.177), channel_id=1, source_target_pairs={{16,0},{32,16},{48,32},{64,48},{80,64},{96,80},{112,96},{128,112},... | collective-permute-start | bytes 1474568 | tf_op jit(solution)/shard_map/ppermute | solution.py:18
  19.7 34.6 %copy-start.2 = (s32[1,256]{1,0:T(1,128)S(1)}, s32[1,256]{1,0:T(1,128)}, u32[]{:S(2)}) copy-start(s32[1,256]{1,0:T(1,128)} %param.18) | copy-start | bytes 3076
  154.8 4.5 collective-permute-start.2
  157.4 5.1 %collective-permute-start.3 = (f32[16,15,128]{2,0,1:T(8,128)S(1)}, f32[16,15,128]{2,0,1:T(8,128)S(1)}, u32[]{:S(2)}, u32[]{:S(2)}) collective-permute-start(f32[16,15,128]{2,0,1:T(8,128)S(1)} %get-tuple-element.175), channel_id=1, source_target_pairs={{4,0},{8,4},{12,8},{0,12},{5,1},{9,5},{13,9},{1,13},{6,2},{10,6},{... | collective-permute-start | bytes 368648 | tf_op jit(solution)/shard_map/ppermute | solution.py:18
  166.6 4.1 copy-start.3
  166.6 21.3 %all-to-all-start = ((f32[16,2,64,128]{3,2,1,0:T(8,128)}), f32[16,2,64,128]{3,2,1,0:T(8,128)S(1)}, u32[]{:S(2)}, u32[]{:S(2)}) async-start(f32[16,2,64,128]{3,2,1,0:T(8,128)} %copy.43), calls=%async_computation | async-start | bytes 2097152 | tf_op jit(solution)/shard_map/all_to_all | solution.py:111
  189.1 47.0 %copy-start = (f32[1,16,64,128]{3,2,1,0:T(8,128)S(1)}, f32[1,16,64,128]{3,2,1,0:T(8,128)}, u32[]{:S(2)}) copy-start(f32[1,16,64,128]{3,2,1,0:T(8,128)} %param.16) | copy-start | bytes 1572868
  286.4 101.2 %all-to-all-start.1 = ((f32[16,2,64,128]{3,2,1,0:T(8,128)}), f32[16,2,64,128]{3,2,1,0:T(8,128)S(1)}, u32[]{:S(2)}, u32[]{:S(2)}) async-start(f32[16,2,64,128]{3,2,1,0:T(8,128)} %copy.49), calls=%async_computation.1 | async-start | bytes 2097152 | tf_op jit(solution)/shard_map/all_to_all | solution.py:111
  290.2 210.4 %all-reduce.2.cloned.1.call-start = ((), (), s32[]{:S(2)}) async-start(), calls=%async_computation.2 | async-start | bytes 1048576 | tf_op jit(solution)/shard_map/psum | solution.py:144
  389.6 37.6 %collective-permute-start.4 = (f32[16,15,128]{2,1,0:T(8,128)S(1)}, f32[16,15,128]{2,1,0:T(8,128)S(1)}, u32[]{:S(2)}, u32[]{:S(2)}) collective-permute-start(f32[16,15,128]{2,1,0:T(8,128)S(1)} %get-tuple-element.172), channel_id=1, source_target_pairs={{0,4},{4,8},{8,12},{12,0},{1,5},{5,9},{9,13},{13,1},{2,6},{6,10},{... | collective-permute-start | bytes 368648 | tf_op jit(solution)/shard_map/ppermute | solution.py:16
  393.2 34.0 %collective-permute-start.5 = (f32[16,15,128]{2,1,0:T(8,128)S(1)}, f32[16,15,128]{2,1,0:T(8,128)S(1)}, u32[]{:S(2)}, u32[]{:S(2)}) collective-permute-start(f32[16,15,128]{2,1,0:T(8,128)S(1)} %get-tuple-element.173), channel_id=1, source_target_pairs={{4,0},{8,4},{12,8},{0,12},{5,1},{9,5},{13,9},{1,13},{6,2},{10,6},{... | collective-permute-start | bytes 368648 | tf_op jit(solution)/shard_map/ppermute | solution.py:18
  428.2 16.5 %collective-permute-start.6 = (f32[15,64,128]{2,1,0:T(8,128)S(1)}, f32[15,64,128]{2,1,0:T(8,128)S(1)}, u32[]{:S(2)}, u32[]{:S(2)}) collective-permute-start(f32[15,64,128]{2,1,0:T(8,128)S(1)} %get-tuple-element.170), channel_id=1, source_target_pairs={{0,16},{16,32},{32,48},{48,64},{64,80},{80,96},{96,112},{112,128},... | collective-permute-start | bytes 1474568 | tf_op jit(solution)/shard_map/ppermute | solution.py:16
  429.8 14.9 %collective-permute-start.7 = (f32[15,64,128]{2,1,0:T(8,128)S(1)}, f32[15,64,128]{2,1,0:T(8,128)S(1)}, u32[]{:S(2)}, u32[]{:S(2)}) collective-permute-start(f32[15,64,128]{2,1,0:T(8,128)S(1)} %get-tuple-element.171), channel_id=1, source_target_pairs={{16,0},{32,16},{48,32},{64,48},{80,64},{96,80},{112,96},{128,112},... | collective-permute-start | bytes 1474568 | tf_op jit(solution)/shard_map/ppermute | solution.py:18
Sparse Core Ops, SparseCore 0:
  447.4 53.1 all-reduce.1
where the time goes:
time: 513 us; the launch traced here: 510 us
  local copies, waits for them, and re-layouts  306 us (60%)
  waiting for transfers between devices  81.3 us (16%)
  loops' own time  67.6 us (13%)
  starting transfers between devices  25.5 us (5%)
  between operations  13.9 us (3%)
  matrix products  12.3 us (2%)
    gather x2, local copies, waits for them, and re-layouts, blur_columns(): weights = jnp.take(padded, jnp.where(inside, offset, tap_count))  194 us
    gather x8, local copies, waits for them, and re-layouts, band_matrix(): return jnp.take(padded, jnp.where(inside, offset, tap_count))  77.7 us
    another operation x2, loops' own time, shear_planes(): return lax.map(one_plane, (doubled, starts))  67.6 us
    psum x1, waiting for transfers between devices, local(): lax.psum(correction, 'view')  53.3 us
    dynamic_slice x32, local copies, waits for them, and re-layouts, shear_planes(): return lax.map(one_plane, (doubled, starts))  21.3 us
    all_to_all x2, waiting for transfers between devices, route_planes(): lax.all_to_all(buffer, 'slab', split_axis=0, concat_axis=0, tiled=True)  17.1 us
  transfers between devices with their start and end apart: 11, of which 5 were waited for; matrix products, arithmetic and copies ran while one was open for 54% of the time, Pallas kernels for 0%

commit v1 on v0

v1 whole, which is shorter than its diff:
```python
import functools

import jax
import jax.numpy as jnp
from jax import lax
from jax.experimental import pallas as pl
from jax.experimental.pallas import tpu as pltpu
from jax.sharding import PartitionSpec as P

MESH = pl.DeviceIdType.MESH
EXACT = lax.Precision.HIGHEST
TAPS = 31
RADIUS = 15
HALO = 16


def dot(a, b):
    return jnp.dot(a, b, precision=EXACT, preferred_element_type=jnp.float32)


def circulant(taps, flip):
    total = taps[0]
    for t in range(1, TAPS):
        total = total + taps[t]
    row = lax.broadcasted_iota(jnp.int32, (128, 128), 0)
    col = lax.broadcasted_iota(jnp.int32, (128, 128), 1)
    off = lax.rem(col - row + RADIUS + 128, 128)
    out = jnp.zeros((128, 128), jnp.float32)
    for t in range(TAPS):
        out = jnp.where(off == t, taps[TAPS - 1 - t if flip else t], out)
    return out / jnp.full((128, 128), total)


def wide(block):
    row = lax.broadcasted_iota(jnp.int32, (128, 128), 0)
    col = lax.broadcasted_iota(jnp.int32, (128, 128), 1)
    near = jnp.abs(row - col) <= RADIUS
    a = jnp.where(near, block, 0.0)
    b = jnp.where(near, 0.0, block)
    return jnp.concatenate(
        [jnp.concatenate([a, b], axis=1), jnp.concatenate([b, a], axis=1)], axis=0
    )


def kernel(
    taps_ref, shift_ref, source_ref, est_ref, meas_ref, out_ref,
    ext, meas, packed_m, packed_e, got_m, got_e, forth, seen, rolled, table, tables,
    edges, arrived, acc, spread, quarter, band_y, mix_x, band_z, back_z, pick, mix_back,
    local_sem, halo_send, halo_recv, tap_send, tap_recv, m_send, m_recv, e_send, e_recv,
    p_send, p_recv, edge_send, edge_recv, ready,
):
    slab, tile, view = lax.axis_index("slab"), lax.axis_index("tile"), lax.axis_index("view")
    side = 4
    sy, sx = slab // side, lax.rem(slab, side)
    up, down = lax.rem(tile + 1, 4), lax.rem(tile + 3, 4)

    def slab_at(d):
        dy, dx = d // side, lax.rem(d, side)
        return lax.rem(sy + dy, side) * side + lax.rem(sx + dx, side)

    def view_at(d):
        return lax.rem(view + d, 4)

    own_est = pltpu.make_async_copy(est_ref, ext.at[:, pl.ds(HALO, 64), :], local_sem.at[0])
    own_meas = pltpu.make_async_copy(meas_ref.at[0], meas, local_sem.at[1])
    own_est.start()
    own_meas.start()

    barrier = pltpu.get_barrier_semaphore()

    def greet(d, _):
        pl.semaphore_signal(
            barrier, inc=1, device_id=(slab_at(d), tile, view), device_id_type=MESH
        )
        return 0

    lax.fori_loop(1, 16, greet, 0)
    for t in (up, down):
        pl.semaphore_signal(barrier, inc=1, device_id=(slab, t, view), device_id_type=MESH)
    for d in (1, 2, 3):
        pl.semaphore_signal(
            barrier, inc=1, device_id=(slab, tile, view_at(d)), device_id_type=MESH
        )

    taps_y = [taps_ref[0, 1, t] for t in range(TAPS)]
    total_y = taps_y[0]
    for t in range(1, TAPS):
        total_y = total_y + taps_y[t]
    for t in range(TAPS):
        table[pl.ds(t, 1), :] = jnp.full((1, 128), taps_y[t])
    table[pl.ds(TAPS, 1), :] = jnp.zeros((1, 128), jnp.float32)
    table[...] = table[...] / jnp.full((32, 128), total_y)

    pl.semaphore_wait(barrier, 20)

    to_up = pltpu.make_async_remote_copy(
        src_ref=est_ref.at[:, pl.ds(64 - HALO, HALO), :], dst_ref=ext.at[:, pl.ds(0, HALO), :],
        send_sem=halo_send.at[0], recv_sem=halo_recv.at[0],
        device_id=(slab, up, view), device_id_type=MESH,
    )
    to_down = pltpu.make_async_remote_copy(
        src_ref=est_ref.at[:, pl.ds(0, HALO), :], dst_ref=ext.at[:, pl.ds(64 + HALO, HALO), :],
        send_sem=halo_send.at[1], recv_sem=halo_recv.at[1],
        device_id=(slab, down, view), device_id_type=MESH,
    )
    to_up.start()
    to_down.start()
    tap_copies = []
    for d in (1, 2, 3):
        c = pltpu.make_async_remote_copy(
            src_ref=table, dst_ref=tables.at[view],
            send_sem=tap_send.at[d], recv_sem=tap_recv.at[d],
            device_id=(slab, tile, view_at(d)), device_id_type=MESH,
        )
        c.start()
        tap_copies.append(c)
        pl.semaphore_signal(
            ready, inc=1, device_id=(slab, tile, view_at(d)), device_id_type=MESH
        )
    tables[view] = table[...]

    own_meas.wait()
    for j in range(16):
        amount = lax.rem(128 - shift_ref[0, slab * 16 + j], 128)
        plane = pltpu.roll(meas[j], amount, 1)
        packed_m[pl.ds(j, 64, stride=16), :] = plane

    def m_copy(d):
        to = slab_at(d)
        return pltpu.make_async_remote_copy(
            src_ref=packed_m3.at[pl.ds(to * 4, 4)],
            dst_ref=got_m.at[:, pl.ds(pl.multiple_of(slab * 16, 16), 16), :],
            send_sem=m_send.at[d], recv_sem=m_recv.at[d],
            device_id=(to, tile, view), device_id_type=MESH,
        )

    def e_copy(d):
        to = slab_at(d)
        return pltpu.make_async_remote_copy(
            src_ref=packed_e3.at[pl.ds(to * 4, 4)],
            dst_ref=got_e.at[:, pl.ds(pl.multiple_of(slab * 16, 16), 16), :],
            send_sem=e_send.at[d], recv_sem=e_recv.at[d],
            device_id=(to, tile, view), device_id_type=MESH,
        )

    packed_m3 = packed_m.reshape(64, 16, 128)
    packed_e3 = packed_e.reshape(64, 16, 128)

    def start_m(d, _):
        m_copy(d).start()
        return 0

    lax.fori_loop(1, 16, start_m, 0)
    mine = pl.ds(pl.multiple_of(slab * 16, 16), 16)
    for k in range(4):
        got_m[k, mine, :] = packed_m3[slab * 4 + k]

    band_y[...] = circulant([taps_ref[0, 1, t] for t in range(TAPS)], False)
    mix_x[...] = circulant([taps_ref[0, 2, t] for t in range(TAPS)], True)

    own_est.wait()
    to_up.wait()
    to_down.wait()
    flat = jnp.concatenate([ext[z] for z in range(16)], axis=1)
    by_y = dot(band_y[HALO : 64 + HALO, 0:96], flat)
    tall = jnp.concatenate([by_y[:, 128 * z : 128 * z + 128] for z in range(16)], axis=0)
    by_x = dot(tall, mix_x[...])
    for z in range(16):
        packed_e[pl.ds(z, 64, stride=16), :] = by_x[64 * z : 64 * z + 64, :]

    def start_e(d, _):
        e_copy(d).start()
        return 0

    lax.fori_loop(1, 16, start_e, 0)
    for k in range(4):
        got_e[k, mine, :] = packed_e3[slab * 4 + k]

    taps_z = [taps_ref[0, 0, t] for t in range(TAPS)]
    band_z[...] = wide(circulant(taps_z, False))
    back_z[...] = wide(circulant(taps_z, True))
    plane_of = lax.broadcasted_iota(jnp.int32, (256, 256), 0)
    pick[...] = (jnp.broadcast_to(source_ref[...], (256, 256)) == plane_of).astype(jnp.float32)
    x_adjoint = circulant([taps_ref[0, 2, t] for t in range(TAPS)], False)
    lane = lax.broadcasted_iota(jnp.int32, (128, 128), 1)
    for k in range(4):
        for w in range(4):
            turned = x_adjoint if k == w else pltpu.roll(x_adjoint, (32 * (k - w)) % 128, 1)
            mix_back[128 * k : 128 * k + 128, 128 * w : 128 * w + 128] = jnp.where(
                (lane >= 32 * k) & (lane < 32 * k + 32), turned, 0.0
            )
    for z in range(16):
        quarter[z] = pltpu.roll(ext[z, HALO : 64 + HALO, :], lax.rem(128 - 32 * view, 128), 1)
    for v in range(4):
        for r in range(4):
            rolled[v, r, 0:8] = jnp.zeros((8, 16, 128), jnp.float32)
            rolled[v, r, 23:31] = jnp.zeros((8, 16, 128), jnp.float32)

    def wait_m(d, _):
        m_copy(d).wait()
        return 0

    lax.fori_loop(1, 16, wait_m, 0)
    routed = dot(pick[...], jnp.concatenate([got_m[k] for k in range(4)], axis=1))

    def wait_e(d, _):
        e_copy(d).wait()
        return 0

    lax.fori_loop(1, 16, wait_e, 0)
    blurred = dot(band_z[...], jnp.concatenate([got_e[k] for k in range(4)], axis=1))
    pulled = dot(back_z[...], routed / blurred)
    by_quarter = dot(pulled, mix_back[...])
    for w in range(4):
        forth[w] = by_quarter[:, 128 * w : 128 * w + 128]

    pl.semaphore_wait(ready, 3)

    def p_copy(ds, dv):
        to, w = slab_at(ds), view_at(dv)
        return pltpu.make_async_remote_copy(
            src_ref=forth.at[w, pl.ds(pl.multiple_of(to * 16, 16), 16), :],
            dst_ref=seen.at[view, slab],
            send_sem=p_send.at[dv, ds], recv_sem=p_recv.at[dv, ds],
            device_id=(to, tile, w), device_id_type=MESH,
        )

    def start_p(ds, _):
        for dv in (2, 1, 3):
            p_copy(ds, dv).start()

        @pl.when(ds > 0)
        def _():
            p_copy(ds, 0).start()

        return 0

    lax.fori_loop(0, 16, start_p, 0)
    seen[view, slab] = forth[view, mine, :]
    for c in tap_copies:
        c.wait()

    def wait_p(ds, _):
        for dv in (2, 1, 3):
            p_copy(ds, dv).wait()

        @pl.when(ds > 0)
        def _():
            p_copy(ds, 0).wait()

        return 0

    lax.fori_loop(0, 16, wait_p, 0)

    lanes = lax.broadcasted_iota(jnp.int32, (16, 16, 128), 2)
    for v in range(4):
        block = seen[v]
        rolled[v, 0, 8:24] = block
        for r in (1, 2, 3):
            turned = pltpu.roll(block.reshape(256, 128), 128 - 32 * r, 1).reshape(16, 16, 128)
            keep = lanes < 128 - 32 * r
            rolled[v, r, 8:24] = jnp.where(keep, turned, 0.0)
            follow = jnp.where(keep, 0.0, turned)
            rolled[v, r, 7:23] = rolled[v, r, 7:23] + follow

    def gather_rows(base, lo, hi):
        total = [jnp.zeros((16, 128), jnp.float32) for _ in range(4)]
        for v in range(4):
            for d in range(lo, hi + 1):
                m, r = d // 4, d % 4
                c = jnp.broadcast_to(tables[v, pl.ds(RADIUS - d, 1), :], (16, 128))
                for j in range(4):
                    total[j] = total[j] + c * rolled[v, r, base + j + m + 8]
        return total

    low = gather_rows(-4, 0, RADIUS)
    high = gather_rows(16, -RADIUS, -1)
    for j in range(4):
        edges[0, j] = low[j]
        edges[1, j] = high[j]
    edge_down = pltpu.make_async_remote_copy(
        src_ref=edges.at[0], dst_ref=arrived.at[0],
        send_sem=edge_send.at[0], recv_sem=edge_recv.at[0],
        device_id=(slab, down, view), device_id_type=MESH,
    )
    edge_up = pltpu.make_async_remote_copy(
        src_ref=edges.at[1], dst_ref=arrived.at[1],
        send_sem=edge_send.at[1], recv_sem=edge_recv.at[1],
        device_id=(slab, up, view), device_id_type=MESH,
    )
    edge_down.start()
    edge_up.start()

    def chunk(c, _):
        rows = gather_rows(c * 4, -RADIUS, RADIUS)
        for j in range(4):
            acc[c * 4 + j] = rows[j]
        return 0

    lax.fori_loop(0, 4, chunk, 0)
    edge_down.wait()
    edge_up.wait()
    acc[12:16] = acc[12:16] + arrived[0]
    acc[0:4] = acc[0:4] + arrived[1]

    for s in range(16):
        rows = acc[s]
        for k in range(4):
            part = rows if k == 0 else pltpu.roll(rows, 128 - 32 * k, 1)
            spread[pl.ds(4 * s + k, 16, stride=64), :] = part
    for z in range(16):
        summed = spread[64 * z : 64 * z + 64, :]
        out_ref[z] = (quarter[z] * summed * 0.25)[:, 0:32]


def local(estimate, measured, psf_taps, plane_source, plane_shift):
    f32 = jnp.float32
    dma = pltpu.SemaphoreType.DMA
    smem = pl.BlockSpec(memory_space=pltpu.SMEM)
    vmem = pl.BlockSpec(memory_space=pltpu.VMEM)
    hbm = pl.BlockSpec(memory_space=pl.ANY)
    return pl.pallas_call(
        kernel,
        name="update",
        out_shape=jax.ShapeDtypeStruct((16, 64, 32), f32),
        in_specs=[smem, smem, vmem, hbm, hbm],
        out_specs=vmem,
        scratch_shapes=[
            pltpu.VMEM((16, 96, 128), f32),
            pltpu.VMEM((16, 64, 128), f32),
            pltpu.VMEM((1024, 128), f32),
            pltpu.VMEM((1024, 128), f32),
            pltpu.VMEM((4, 256, 128), f32),
            pltpu.VMEM((4, 256, 128), f32),
            pltpu.VMEM((4, 256, 128), f32),
            pltpu.VMEM((4, 16, 16, 128), f32),
            pltpu.VMEM((4, 4, 31, 16, 128), f32),
            pltpu.VMEM((32, 128), f32),
            pltpu.VMEM((4, 32, 128), f32),
            pltpu.VMEM((2, 4, 16, 128), f32),
            pltpu.VMEM((2, 4, 16, 128), f32),
            pltpu.VMEM((16, 16, 128), f32),
            pltpu.VMEM((1024, 128), f32),
            pltpu.VMEM((16, 64, 128), f32),
            pltpu.VMEM((128, 128), f32),
            pltpu.VMEM((128, 128), f32),
            pltpu.VMEM((256, 256), f32),
            pltpu.VMEM((256, 256), f32),
            pltpu.VMEM((256, 256), f32),
            pltpu.VMEM((512, 512), f32),
            dma((2,)), dma((2,)), dma((2,)), dma((4,)), dma((4,)),
            dma((16,)), dma((16,)), dma((16,)), dma((16,)),
            dma((4, 16)), dma((4, 16)), dma((2,)), dma((2,)),
            pltpu.SemaphoreType.REGULAR,
        ],
        compiler_params=pltpu.CompilerParams(
            collective_id=0, has_side_effects=True, vmem_limit_bytes=56 * 2**20
        ),
    )(psf_taps, plane_shift, plane_source, estimate, measured)


def solution(mesh):
    in_specs = (
        P("slab", "tile", None),
        P("view", "slab", "tile", None),
        P("view", None, None),
        P("view", None),
        P("view", None),
    )
    return jax.shard_map(
        local, mesh=mesh, in_specs=in_specs, out_specs=P("slab", "tile", "view"), check_vma=False
    )
```

time: 513 us -> 55 us (0.11)
  local copies, waits for them, and re-layouts: 306 us -> 3.2 us
  waiting for transfers between devices: 81.3 us -> 0 us
  loops' own time: 67.6 us -> 0 us
  Pallas kernels: 0 us -> 51.7 us
  starting transfers between devices: 25.5 us -> 0 us
  between operations: 13.9 us -> 0.01 us
  matrix products: 12.3 us -> 0 us
    gather x10 -> x0, local copies, waits for them, and re-layouts: 272 us -> none  [the longest x2 194 us: blur_columns(): weights = jnp.take(padded, jnp.where(inside, offset, tap_count))]
    another operation x2 -> x0, loops' own time: 67.6 us -> none  [shear_planes(): return lax.map(one_plane, (doubled, starts))]
    psum x1 -> x0, waiting for transfers between devices: 53.3 us -> none  [local(): lax.psum(correction, 'view')]
    pallas_call x0 -> x1, Pallas kernels: none -> 51.7 us  [local(): pl.pallas_call(kernel, name='update', out_shape=jax.ShapeDtypeStruct((16,...]
    dynamic_slice x64 -> x0, local copies, waits for them, and re-layouts: 24.8 us -> none  [the longest x32 21.3 us: shear_planes(): return lax.map(one_plane, (doubled, starts))]
    ppermute x8 -> x0, starting transfers between devices: 17.8 us -> none  [the longest x4 9.95 us: extended_2(): lax.ppermute(tail, axis, [(i, (i + 1) % count) for i in range(count)])]
    all_to_all x2 -> x0, waiting for transfers between devices: 17.1 us -> none  [route_planes(): lax.all_to_all(buffer, 'slab', split_axis=0, concat_axis=0, tiled=True)]
    dot_general x11 -> x0, matrix products: 12.3 us -> none  [the longest x2 4.54 us: apply_depth(): return jnp.einsum('ij,jab->iab', band_rows, extended, precision=exact_mode)]
  transfers between devices with their start and end apart: 11 -> 0, of which waited for: 5 -> 0; matrix products, arithmetic and copies ran while one was open for 54% -> 0% of each run, Pallas kernels for 0% -> 0%
where the time goes in v1:
time: 55 us; the launch traced here: 54.9 us
  Pallas kernels  51.7 us (94%)
  local copies, waits for them, and re-layouts  3.2 us (6%)
    pallas_call x1, Pallas kernels, local(): pl.pallas_call(kernel, name='update', out_shape=jax.ShapeDtypeStruct((16,...  51.7 us
    pallas_call x1, local copies, waits for them, and re-layouts, local(): pl.pallas_call(kernel, name='update', out_shape=jax.ShapeDtypeStruct((16,...  1.94 us
    unnamed x1, local copies, waits for them, and re-layouts  1.26 us

profile of v1, /device:TPU:1, one launch (start us, length us, event | category | flops | bytes accessed | tf_op | source)
XLA Modules:
  0.0 54.9 jit_solution(8186449328169737490)
XLA Ops:
  0.0 1.3 %copy.6.taps_ref = f32[1,3,31]{2,1,0:T(4,128)} copy(f32[1,3,31]{2,0,1:T(1,128)} %param.7) | data formatting | bytes 744 | tf_op args[2]
  1.3 51.7 %update.1 = f32[16,64,32]{2,1,0:T(8,128)} custom-call(f32[1,3,31]{2,1,0:T(4,128)} %copy.6.taps_ref, s32[1,256]{1,0:T(1,128)} %shift_ref.1, s32[1,256]{1,0:T(1,128)} %source_ref.1, f32[16,64,128]{2,1,0:T(8,128)} %est_ref.1, f32[1,16,64,128]{3,2,1,0:T(8,128)} %meas_ref.1), custom_call_target="tpu_custom_call" | custom-call | tf_op jit(solution)/shard_map/update/pallas_call | solution.py:322
  52.9 1.9 %copy.7 = f32[16,64,32]{1,2,0:T(8,128)} copy(f32[16,64,32]{2,1,0:T(8,128)} %update.1) | data formatting | bytes 262144 | tf_op jit(solution)/shard_map/update/pallas_call | solution.py:322

commit v2 on v1

v2 whole, which is shorter than its diff:
```python
import jax
import jax.numpy as jnp
from jax import lax
from jax.experimental import pallas as pl
from jax.experimental.pallas import tpu as pltpu
from jax.sharding import PartitionSpec as P

MESH = pl.DeviceIdType.MESH
F32 = jnp.float32
B16 = jnp.bfloat16
TAPS = 31
RADIUS = 15
HALO = 16


def split(x):
    high = x.astype(B16)
    return high, (x - high.astype(F32)).astype(B16)


def left3(x):
    high, low = split(x)
    return jnp.concatenate([high, high, low], axis=1)


def right3(x):
    high, low = split(x)
    return jnp.concatenate([high, low, high], axis=0)


def dot(a, b):
    return jnp.dot(a, b, preferred_element_type=F32)


def circulant(taps, flip):
    total = taps[0]
    for t in range(1, TAPS):
        total = total + taps[t]
    row = lax.broadcasted_iota(jnp.int32, (128, 128), 0)
    col = lax.broadcasted_iota(jnp.int32, (128, 128), 1)
    off = lax.rem(col - row + RADIUS + 128, 128)
    out = jnp.zeros((128, 128), F32)
    for t in range(TAPS):
        out = jnp.where(off == t, taps[TAPS - 1 - t if flip else t], out)
    return out / jnp.full((128, 128), total)


def wide(block):
    row = lax.broadcasted_iota(jnp.int32, (128, 128), 0)
    col = lax.broadcasted_iota(jnp.int32, (128, 128), 1)
    near = jnp.abs(row - col) <= RADIUS
    a = jnp.where(near, block, 0.0)
    b = jnp.where(near, 0.0, block)
    return jnp.concatenate(
        [jnp.concatenate([a, b], axis=1), jnp.concatenate([b, a], axis=1)], axis=0
    )


def kernel(
    taps_ref, shift_ref, source_ref, est_ref, meas_ref, out_ref,
    ext, meas, pack_m, pack_e, got_m, got_e, forth, seen, table, tables, coefs,
    sums, edges, arrived, final, quarter, band_y, mix_x, band_z, back_z, pick, mix_back,
    local_sem, halo_send, halo_recv, tap_send, tap_recv, m_send, m_recv, e_send, e_recv,
    p_send, p_recv, edge_send, edge_recv, ready,
):
    slab, tile, view = lax.axis_index("slab"), lax.axis_index("tile"), lax.axis_index("view")
    side = 4
    sy, sx = slab // side, lax.rem(slab, side)
    up, down = lax.rem(tile + 1, 4), lax.rem(tile + 3, 4)

    def slab_at(d):
        dy, dx = d // side, lax.rem(d, side)
        return lax.rem(sy + dy, side) * side + lax.rem(sx + dx, side)

    def view_at(d):
        return lax.rem(view + d, 4)

    own_est = pltpu.make_async_copy(est_ref, ext.at[:, pl.ds(HALO, 64), :], local_sem.at[0])
    own_meas = pltpu.make_async_copy(meas_ref.at[0], meas, local_sem.at[1])
    own_est.start()
    own_meas.start()

    barrier = pltpu.get_barrier_semaphore()
    for d in (2, 1, 3):
        pl.semaphore_signal(
            barrier, inc=1, device_id=(slab, tile, view_at(d)), device_id_type=MESH
        )

    def greet(d, _):
        pl.semaphore_signal(
            barrier, inc=1, device_id=(slab_at(d), tile, view), device_id_type=MESH
        )
        return 0

    lax.fori_loop(1, 16, greet, 0)
    for t in (up, down):
        pl.semaphore_signal(barrier, inc=1, device_id=(slab, t, view), device_id_type=MESH)

    taps_z = [taps_ref[0, 0, t] for t in range(TAPS)]
    taps_y = [taps_ref[1, 0, t] for t in range(TAPS)]
    taps_x = [taps_ref[2, 0, t] for t in range(TAPS)]
    total_y = taps_y[0]
    for t in range(1, TAPS):
        total_y = total_y + taps_y[t]
    for t in range(TAPS):
        table[pl.ds(t, 1), :] = jnp.full((1, 128), taps_y[t])
    table[pl.ds(TAPS, 1), :] = jnp.zeros((1, 128), F32)
    table[...] = table[...] / jnp.full((32, 128), total_y)
    tables[view] = table[...]

    band_y[...] = circulant(taps_y, False)
    mix_x[...] = right3(circulant(taps_x, True))

    own_meas.wait()
    for j in range(16):
        amount = lax.rem(128 - shift_ref[0, slab * 16 + j], 128)
        plane = pltpu.roll(meas[j], amount, 1)
        pack_m[0, pl.ds(j, 32, stride=16), :] = plane[16:48]
        pack_m[1, pl.ds(j, 16, stride=16), :] = plane[0:16]
        pack_m[1, pl.ds(256 + j, 16, stride=16), :] = plane[48:64]

    def blur_rows(chunk, band, flat):
        by_y = dot(left3(band), right3(flat))
        tall = jnp.concatenate([by_y[:, 128 * z : 128 * z + 128] for z in range(16)], axis=0)
        by_x = dot(left3(tall), mix_x[...])
        for z in range(16):
            pack_e[chunk, pl.ds(z, 32, stride=16), :] = by_x[32 * z : 32 * z + 32, :]

    own_est.wait()
    blur_rows(
        0,
        band_y[32:64, 16:80],
        jnp.concatenate([ext[z, HALO : 64 + HALO, :] for z in range(16)], axis=1),
    )

    pl.semaphore_wait(barrier, 20)

    to_up = pltpu.make_async_remote_copy(
        src_ref=est_ref.at[:, pl.ds(64 - HALO, HALO), :], dst_ref=ext.at[:, pl.ds(0, HALO), :],
        send_sem=halo_send.at[0], recv_sem=halo_recv.at[0],
        device_id=(slab, up, view), device_id_type=MESH,
    )
    to_down = pltpu.make_async_remote_copy(
        src_ref=est_ref.at[:, pl.ds(0, HALO), :], dst_ref=ext.at[:, pl.ds(64 + HALO, HALO), :],
        send_sem=halo_send.at[1], recv_sem=halo_recv.at[1],
        device_id=(slab, down, view), device_id_type=MESH,
    )
    to_up.start()
    to_down.start()

    mine = pl.ds(pl.multiple_of(slab * 16, 16), 16)
    pack_m5 = pack_m.reshape(2, 2, 16, 16, 128)
    pack_e5 = pack_e.reshape(2, 2, 16, 16, 128)

    def m_copy(chunk, d):
        to = slab_at(d)
        return pltpu.make_async_remote_copy(
            src_ref=pack_m5.at[chunk, :, to], dst_ref=got_m.at[chunk, :, mine, :],
            send_sem=m_send.at[chunk, d], recv_sem=m_recv.at[chunk, d],
            device_id=(to, tile, view), device_id_type=MESH,
        )

    def e_copy(chunk, d):
        to = slab_at(d)
        return pltpu.make_async_remote_copy(
            src_ref=pack_e5.at[chunk, :, to], dst_ref=got_e.at[chunk, :, mine, :],
            send_sem=e_send.at[chunk, d], recv_sem=e_recv.at[chunk, d],
            device_id=(to, tile, view), device_id_type=MESH,
        )

    def exchange(copy, pack, got, chunk):
        def start(d, _):
            copy(chunk, d).start()
            return 0

        lax.fori_loop(1, 16, start, 0)
        for k in range(2):
            got[chunk, k, mine, :] = pack[chunk, k, slab]

    def await_all(copy, chunk):
        def wait(d, _):
            copy(chunk, d).wait()
            return 0

        lax.fori_loop(1, 16, wait, 0)

    exchange(m_copy, pack_m5, got_m, 0)
    exchange(e_copy, pack_e5, got_e, 0)
    tap_copies = []
    for d in (2, 1, 3):
        c = pltpu.make_async_remote_copy(
            src_ref=table, dst_ref=tables.at[view],
            send_sem=tap_send.at[d], recv_sem=tap_recv.at[d],
            device_id=(slab, tile, view_at(d)), device_id_type=MESH,
        )
        c.start()
        tap_copies.append(c)
        pl.semaphore_signal(
            ready, inc=1, device_id=(slab, tile, view_at(d)), device_id_type=MESH
        )
    exchange(m_copy, pack_m5, got_m, 1)

    band_z[...] = left3(wide(circulant(taps_z, False)))
    back_z[...] = left3(wide(circulant(taps_z, True)))
    plane_of = lax.broadcasted_iota(jnp.int32, (256, 256), 0)
    shown = jnp.where(jnp.broadcast_to(source_ref[...], (256, 256)) == plane_of, 1.0, 0.0)
    shown = shown.astype(B16)
    pick[...] = jnp.concatenate([shown, shown], axis=1)
    x_high, x_low = split(circulant(taps_x, False))
    x_high, x_low = x_high.astype(F32), x_low.astype(F32)
    lane = lax.broadcasted_iota(jnp.int32, (128, 128), 1)
    for b in range(4):
        inside = (lane >= 32 * b) & (lane < 32 * b + 32)
        for w in range(4):
            for part, rows in ((x_high, (0, 1024)), (x_low, (512,))):
                turned = part if b == w else pltpu.roll(part, (32 * (b - w)) % 128, 1)
                block = jnp.where(inside, turned, 0.0).astype(B16)
                for row in rows:
                    at = row + 128 * b
                    mix_back[at : at + 128, 128 * w : 128 * w + 128] = block

    to_up.wait()
    to_down.wait()
    blur_rows(
        1,
        jnp.concatenate([band_y[16:32, 0:96], band_y[64:80, 0:96]], axis=0),
        jnp.concatenate([ext[z] for z in range(16)], axis=1),
    )
    exchange(e_copy, pack_e5, got_e, 1)

    def p_copy(chunk, ds, dv):
        to, w = slab_at(ds), view_at(dv)
        return pltpu.make_async_remote_copy(
            src_ref=forth.at[chunk, w, to], dst_ref=seen.at[chunk, view, slab],
            send_sem=p_send.at[chunk, dv, ds], recv_sem=p_recv.at[chunk, dv, ds],
            device_id=(to, tile, w), device_id_type=MESH,
        )

    def process(chunk):
        await_all(m_copy, chunk)
        m = jnp.concatenate([got_m[chunk, 0], got_m[chunk, 1]], axis=1)
        m_high, m_low = split(m)
        routed = dot(pick[...], jnp.concatenate([m_high, m_low], axis=0))
        await_all(e_copy, chunk)
        e = jnp.concatenate([got_e[chunk, 0], got_e[chunk, 1]], axis=1)
        blurred = dot(band_z[...], right3(e))
        pulled = dot(back_z[...], right3(routed / blurred)).reshape(16, 2, 8, 256)
        halves = jnp.concatenate(
            [pulled[:, 0].reshape(128, 256), pulled[:, 1].reshape(128, 256)], axis=1
        )
        by_quarter = dot(left3(halves), mix_back[...])
        for w in range(4):
            forth[chunk, w] = by_quarter[:, 128 * w : 128 * w + 128].reshape(16, 8, 128)
        if chunk == 0:
            pl.semaphore_wait(ready, 3)

        def start(i, _):
            ds = lax.rem(i, 16)
            for dv in (2, 1, 3):
                p_copy(chunk, ds, dv).start()
            return 0

        def start_own(ds, _):
            p_copy(chunk, ds, 0).start()
            return 0

        lax.fori_loop(1, 17, start, 0)
        lax.fori_loop(1, 16, start_own, 0)
        seen[chunk, view, slab] = forth[chunk, view, slab]

    process(0)
    process(1)

    for z in range(16):
        quarter[z] = jnp.transpose(ext[z, HALO : 64 + HALO, :])
    for c in tap_copies:
        c.wait()
    for v in range(4):
        for t in range(TAPS):
            coefs[v, t] = jnp.broadcast_to(tables[v, pl.ds(t, 1), :], (8, 128))

    def await_view(chunk, dv):
        def wait(ds, _):
            p_copy(chunk, ds, dv).wait()
            return 0

        lax.fori_loop(1, 16, wait, 0)
        if dv:
            p_copy(chunk, 0, dv).wait()

    def accumulate(chunk, dv, kind):
        v = lax.rem(view + 4 - dv, 4)
        shift = (0, 16, -16)[kind]
        for s in range(16):
            total = sums[chunk, kind, s] if dv else None
            for source in range(16):
                d = source + shift - s
                if abs(d) <= RADIUS:
                    term = coefs[v, RADIUS - d] * seen[chunk, v, source]
                    total = term if total is None else total + term
            if total is not None:
                sums[chunk, kind, s] = total

    sums[0, 1, 0] = jnp.zeros((8, 128), F32)
    sums[1, 1, 0] = jnp.zeros((8, 128), F32)
    sums[0, 2, 15] = jnp.zeros((8, 128), F32)
    sums[1, 2, 15] = jnp.zeros((8, 128), F32)
    for chunk in range(2):
        for dv in (0, 2, 1, 3):
            await_view(chunk, dv)
            accumulate(chunk, dv, 1)
            accumulate(chunk, dv, 2)
            if (chunk, dv) != (1, 3):
                accumulate(chunk, dv, 0)

    even = lax.rem(lax.broadcasted_iota(jnp.int32, (8, 128), 1) // 32, 2) == 0
    for s in range(8):
        edges[0, s] = jnp.where(even, sums[1, 1, s + 8], pltpu.roll(sums[1, 1, s], 32, 1))
        edges[1, s] = jnp.where(even, pltpu.roll(sums[1, 2, s], 96, 1), sums[1, 2, s + 8])
    edge_down = pltpu.make_async_remote_copy(
        src_ref=edges.at[0], dst_ref=arrived.at[0],
        send_sem=edge_send.at[0], recv_sem=edge_recv.at[0],
        device_id=(slab, down, view), device_id_type=MESH,
    )
    edge_up = pltpu.make_async_remote_copy(
        src_ref=edges.at[1], dst_ref=arrived.at[1],
        send_sem=edge_send.at[1], recv_sem=edge_recv.at[1],
        device_id=(slab, up, view), device_id_type=MESH,
    )
    edge_down.start()
    edge_up.start()
    accumulate(1, 3, 0)
    for s in range(16):
        above_0, above_1 = sums[0, 1, s], sums[1, 1, s]
        below_0, below_1 = sums[0, 2, s], sums[1, 2, s]
        final[0, s] = sums[0, 0, s] + jnp.where(
            even,
            pltpu.roll(above_0, 96, 1) + below_1,
            above_1 + pltpu.roll(below_0, 32, 1),
        )
        final[1, s] = sums[1, 0, s] + jnp.where(even, above_0, below_0)
    edge_down.wait()
    edge_up.wait()
    for s in range(8):
        from_up, from_down = arrived[0, s], arrived[1, s]
        final[1, s] = final[1, s] + jnp.where(even, from_down, from_up)
        final[1, s + 8] = final[1, s + 8] + jnp.where(
            even, pltpu.roll(from_down, 96, 1), pltpu.roll(from_up, 32, 1)
        )

    low = lax.broadcasted_iota(jnp.int32, (32, 64), 1) < 32
    own_x = pl.ds(pl.multiple_of(view * 32, 32), 32)
    for z in range(8):
        a, b = final[0, :, z, :], final[1, :, z, :]
        turned = jnp.transpose(jnp.concatenate([b, a, a, b], axis=0))
        for half in range(2):
            at = 64 * half
            summed = jnp.where(low, turned[at : at + 32], turned[at + 32 : at + 64])
            out_ref[8 * half + z] = quarter[8 * half + z, own_x, :] * summed * 0.25


def local(estimate, measured, psf_taps, plane_source, plane_shift):
    dma = pltpu.SemaphoreType.DMA
    smem = pl.BlockSpec(memory_space=pltpu.SMEM)
    vmem = pl.BlockSpec(memory_space=pltpu.VMEM)
    hbm = pl.BlockSpec(memory_space=pl.ANY)
    out = pl.pallas_call(
        kernel,
        name="update",
        out_shape=jax.ShapeDtypeStruct((16, 32, 64), F32),
        in_specs=[smem, smem, vmem, hbm, hbm],
        out_specs=vmem,
        scratch_shapes=[
            pltpu.VMEM((16, 96, 128), F32),
            pltpu.VMEM((16, 64, 128), F32),
            pltpu.VMEM((2, 512, 128), F32),
            pltpu.VMEM((2, 512, 128), F32),
            pltpu.VMEM((2, 2, 256, 128), F32),
            pltpu.VMEM((2, 2, 256, 128), F32),
            pltpu.VMEM((2, 4, 16, 8, 128), F32),
            pltpu.VMEM((2, 4, 16, 8, 128), F32),
            pltpu.VMEM((32, 128), F32),
            pltpu.VMEM((4, 32, 128), F32),
            pltpu.VMEM((4, 32, 8, 128), F32),
            pltpu.VMEM((2, 3, 16, 8, 128), F32),
            pltpu.VMEM((2, 8, 8, 128), F32),
            pltpu.VMEM((2, 8, 8, 128), F32),
            pltpu.VMEM((2, 16, 8, 128), F32),
            pltpu.VMEM((16, 128, 64), F32),
            pltpu.VMEM((128, 128), F32),
            pltpu.VMEM((384, 128), B16),
            pltpu.VMEM((256, 768), B16),
            pltpu.VMEM((256, 768), B16),
            pltpu.VMEM((256, 512), B16),
            pltpu.VMEM((1536, 512), B16),
            dma((2,)), dma((2,)), dma((2,)), dma((4,)), dma((4,)),
            dma((2, 16)), dma((2, 16)), dma((2, 16)), dma((2, 16)),
            dma((2, 4, 16)), dma((2, 4, 16)), dma((2,)), dma((2,)),
            pltpu.SemaphoreType.REGULAR,
        ],
        compiler_params=pltpu.CompilerParams(
            collective_id=0, has_side_effects=True, vmem_limit_bytes=56 * 2**20
        ),
    )(jnp.transpose(psf_taps, (1, 0, 2)), plane_shift, plane_source, estimate, measured)
    return jnp.transpose(out, (0, 2, 1))


def solution(mesh):
    in_specs = (
        P("slab", "tile", None),
        P("view", "slab", "tile", None),
        P("view", None, None),
        P("view", None),
        P("view", None),
    )
    return jax.shard_map(
        local, mesh=mesh, in_specs=in_specs, out_specs=P("slab", "tile", "view"), check_vma=False
    )
```

time: 55 us -> 46.9 us (0.85)
  Pallas kernels: 51.7 us -> 45.1 us
  local copies, waits for them, and re-layouts: 3.2 us -> 1.67 us
    pallas_call x1, Pallas kernels: 51.7 us -> 45.1 us  [local(): pl.pallas_call(kernel, name='update', out_shape=jax.ShapeDtypeStruct((16,...]
    pallas_call x1 -> x0, local copies, waits for them, and re-layouts: 1.94 us -> none  [local(): pl.pallas_call(kernel, name='update', out_shape=jax.ShapeDtypeStruct((16,...]
where the time goes in v2:
time: 46.9 us; the launch traced here: 46.8 us
  Pallas kernels  45.1 us (96%)
  local copies, waits for them, and re-layouts  1.67 us (4%)
    pallas_call x1, Pallas kernels, local(): pl.pallas_call(kernel, name='update', out_shape=jax.ShapeDtypeStruct((16,...  45.1 us
    unnamed x1, local copies, waits for them, and re-layouts  1.67 us

profile of v2, /device:TPU:1, one launch (start us, length us, event | category | flops | bytes accessed | tf_op | source)
XLA Modules:
  0.0 46.8 jit_solution(1213769437754297210)
XLA Ops:
  0.0 45.1 %update.1 = f32[16,32,64]{2,1,0:T(8,128)} custom-call(f32[3,1,31]{2,1,0:T(1,128)} %bitcast.3, s32[1,256]{1,0:T(1,128)} %shift_ref.1, s32[1,256]{1,0:T(1,128)} %source_ref.1, f32[16,64,128]{2,1,0:T(8,128)} %est_ref.1, f32[1,16,64,128]{3,2,1,0:T(8,128)} %meas_ref.1), custom_call_target="tpu_custom_call" | custom-call | tf_op jit(solution)/shard_map/update/pallas_call | solution.py:367
  45.1 1.7 %copy.7 = f32[16,64,32]{1,2,0:T(8,128)} copy(f32[16,64,32]{1,2,0:T(8,128)} %bitcast.2) | data formatting | bytes 262144

commit v3 on v2

v3 whole, which is shorter than its diff:
```python
import jax
import jax.numpy as jnp
from jax import lax
from jax.experimental import pallas as pl
from jax.experimental.pallas import tpu as pltpu
from jax.sharding import PartitionSpec as P

MESH = pl.DeviceIdType.MESH
F32 = jnp.float32
B16 = jnp.bfloat16
TAPS = 31
RADIUS = 15
HALO = 16


def split(x):
    high = x.astype(B16)
    return high, (x - high.astype(F32)).astype(B16)


def left3(x):
    high, low = split(x)
    return jnp.concatenate([high, high, low], axis=1)


def right3(x):
    high, low = split(x)
    return jnp.concatenate([high, low, high], axis=0)


def dot(a, b):
    return jnp.dot(a, b, preferred_element_type=F32)


def circulant(taps, flip):
    total = taps[0]
    for t in range(1, TAPS):
        total = total + taps[t]
    row = lax.broadcasted_iota(jnp.int32, (128, 128), 0)
    col = lax.broadcasted_iota(jnp.int32, (128, 128), 1)
    off = lax.rem(col - row + RADIUS + 128, 128)
    out = jnp.zeros((128, 128), F32)
    for t in range(TAPS):
        out = jnp.where(off == t, taps[TAPS - 1 - t if flip else t], out)
    return out / jnp.full((128, 128), total)


def wide(block):
    row = lax.broadcasted_iota(jnp.int32, (128, 128), 0)
    col = lax.broadcasted_iota(jnp.int32, (128, 128), 1)
    near = jnp.abs(row - col) <= RADIUS
    a = jnp.where(near, block, 0.0)
    b = jnp.where(near, 0.0, block)
    return jnp.concatenate(
        [jnp.concatenate([a, b], axis=1), jnp.concatenate([b, a], axis=1)], axis=0
    )


ORDER = (1, 0, 3, 2)
FAR_FIRST = (10, 6, 14, 9, 11, 2, 8, 5, 7, 13, 15, 1, 3, 4, 12)


def kernel(
    taps_ref, shift_ref, source_ref, est_ref, meas_ref, out_ref,
    ext, meas, pack_m, pack_e, got_m, got_e, forth, seen, table, tables, coefs,
    final, edges, arrived, quarter, band_y, mix_x, band_z, natural, back_z, pick, back_x,
    local_sem, halo_send, halo_recv, tap_send, tap_recv, m_send, m_recv, e_send, e_recv,
    gauge, p_send, p_recv, edge_send, edge_recv, ready,
):
    slab, tile, view = lax.axis_index("slab"), lax.axis_index("tile"), lax.axis_index("view")
    side = 4
    sy, sx = slab // side, lax.rem(slab, side)
    up, down = lax.rem(tile + 1, 4), lax.rem(tile + 3, 4)

    def slab_at(d):
        dy, dx = d // side, lax.rem(d, side)
        return lax.rem(sy + dy, side) * side + lax.rem(sx + dx, side)

    def view_at(d):
        return lax.rem(view + d, 4)

    own_est = pltpu.make_async_copy(est_ref, ext.at[:, pl.ds(HALO, 64), :], local_sem.at[0])
    own_meas = pltpu.make_async_copy(meas_ref.at[0], meas, local_sem.at[1])
    own_est.start()
    own_meas.start()

    barrier = pltpu.get_barrier_semaphore()
    pl.semaphore_signal(barrier, inc=1, device_id=(slab, tile, view_at(2)), device_id_type=MESH)
    for d in FAR_FIRST:
        pl.semaphore_signal(
            barrier, inc=1, device_id=(slab_at(d), tile, view), device_id_type=MESH
        )
    for d in (1, 3):
        pl.semaphore_signal(
            barrier, inc=1, device_id=(slab, tile, view_at(d)), device_id_type=MESH
        )
    for t in (up, down):
        pl.semaphore_signal(barrier, inc=1, device_id=(slab, t, view), device_id_type=MESH)

    taps_z = [taps_ref[0, 0, t] for t in range(TAPS)]
    taps_y = [taps_ref[1, 0, t] for t in range(TAPS)]
    taps_x = [taps_ref[2, 0, t] for t in range(TAPS)]
    total_y = taps_y[0]
    for t in range(1, TAPS):
        total_y = total_y + taps_y[t]
    for t in range(TAPS):
        table[pl.ds(t, 1), :] = jnp.full((1, 128), taps_y[t])
    table[pl.ds(TAPS, 1), :] = jnp.zeros((1, 128), F32)
    table[...] = table[...] / jnp.full((32, 128), total_y)
    tables[view] = table[...]

    band_y[...] = circulant(taps_y, False)
    mix_x[...] = right3(circulant(taps_x, True))

    own_meas.wait()
    for j in range(16):
        amount = lax.rem(128 - shift_ref[0, slab * 16 + j], 128)
        plane = pltpu.roll(meas[j], amount, 1)
        for chunk, k in enumerate(ORDER):
            pack_m[chunk, pl.ds(j, 16, stride=16), :] = plane[16 * k : 16 * k + 16]

    def blur_rows(chunks, band, flat):
        by_y = dot(left3(band), right3(flat))
        tall = jnp.concatenate([by_y[:, 128 * z : 128 * z + 128] for z in range(16)], axis=0)
        by_x = dot(left3(tall), mix_x[...])
        for z in range(16):
            for i, chunk in enumerate(chunks):
                at = 32 * z + 16 * i
                pack_e[chunk, pl.ds(z, 16, stride=16), :] = by_x[at : at + 16, :]

    own_est.wait()
    blur_rows(
        (0, 3),
        band_y[32:64, 16:80],
        jnp.concatenate([ext[z, HALO : 64 + HALO, :] for z in range(16)], axis=1),
    )

    pl.semaphore_wait(barrier, 20)

    to_up = pltpu.make_async_remote_copy(
        src_ref=est_ref.at[:, pl.ds(64 - HALO, HALO), :], dst_ref=ext.at[:, pl.ds(0, HALO), :],
        send_sem=halo_send.at[0], recv_sem=halo_recv.at[0],
        device_id=(slab, up, view), device_id_type=MESH,
    )
    to_down = pltpu.make_async_remote_copy(
        src_ref=est_ref.at[:, pl.ds(0, HALO), :], dst_ref=ext.at[:, pl.ds(64 + HALO, HALO), :],
        send_sem=halo_send.at[1], recv_sem=halo_recv.at[1],
        device_id=(slab, down, view), device_id_type=MESH,
    )
    to_up.start()
    to_down.start()

    mine = pl.ds(pl.multiple_of(slab * 16, 16), 16)

    def exchange(chunk, pack, got, send, recv):
        def start(d, _):
            to = slab_at(d)
            pltpu.make_async_remote_copy(
                src_ref=pack.at[chunk, pl.ds(pl.multiple_of(to * 16, 16), 16), :],
                dst_ref=got.at[chunk, mine, :],
                send_sem=send.at[chunk], recv_sem=recv.at[chunk],
                device_id=(to, tile, view), device_id_type=MESH,
            ).start()
            return 0

        lax.fori_loop(1, 16, start, 0)
        got[chunk, mine, :] = pack[chunk, mine, :]

    def await_bytes(ref, sem):
        pltpu.make_async_copy(ref, ref, sem).wait()

    def exchange_m(chunk):
        exchange(chunk, pack_m, got_m, m_send, m_recv)

    def exchange_e(chunk):
        exchange(chunk, pack_e, got_e, e_send, e_recv)

    exchange_m(0)
    exchange_e(0)
    tap_copies = []
    for d in (2, 1, 3):
        c = pltpu.make_async_remote_copy(
            src_ref=table, dst_ref=tables.at[view],
            send_sem=tap_send.at[d], recv_sem=tap_recv.at[d],
            device_id=(slab, tile, view_at(d)), device_id_type=MESH,
        )
        c.start()
        tap_copies.append(c)
        pl.semaphore_signal(
            ready, inc=1, device_id=(slab, tile, view_at(d)), device_id_type=MESH
        )
    exchange_m(1)
    exchange_m(2)

    band_z[...] = left3(wide(circulant(taps_z, False)))
    natural[...] = wide(circulant(taps_z, True))
    for zq in range(4):
        rows = jnp.concatenate(
            [natural[16 * s + 4 * zq : 16 * s + 4 * zq + 4, :] for s in range(16)], axis=0
        )
        back_z[64 * zq : 64 * zq + 64, :] = left3(rows)
    plane_of = lax.broadcasted_iota(jnp.int32, (256, 256), 0)
    shown = jnp.where(jnp.broadcast_to(source_ref[...], (256, 256)) == plane_of, 1.0, 0.0)
    shown = shown.astype(B16)
    pick[...] = jnp.concatenate([shown, shown], axis=1)
    back_x[...] = right3(circulant(taps_x, False))
    final[...] = jnp.zeros_like(final)
    edges[...] = jnp.zeros_like(edges)

    to_up.wait()
    to_down.wait()
    blur_rows(
        (1, 2),
        jnp.concatenate([band_y[16:32, 0:96], band_y[64:80, 0:96]], axis=0),
        jnp.concatenate([ext[z] for z in range(16)], axis=1),
    )
    exchange_e(1)
    exchange_e(2)

    block = lax.broadcasted_iota(jnp.int32, (64, 128), 1) // 32
    half = pl.ds(pl.multiple_of(lax.rem(slab, 2) * 4, 4), 4)

    def process(chunk):
        await_bytes(got_m.at[chunk, pl.ds(0, 240)], m_recv.at[chunk])
        m_high, m_low = split(got_m[chunk])
        routed = dot(pick[...], jnp.concatenate([m_high, m_low], axis=0))
        await_bytes(got_e.at[chunk, pl.ds(0, 240)], e_recv.at[chunk])
        blurred = dot(band_z[...], right3(got_e[chunk]))
        pulled = dot(back_z[...], right3(routed / blurred))
        by_x = dot(left3(pulled), back_x[...])
        turned = [by_x] + [pltpu.roll(by_x, 32 * m, 1) for m in (1, 2, 3)]
        for w in range(4):
            out = turned[(3 - w) % 4][192:256]
            for zq in (2, 1, 0):
                out = jnp.where(block == zq, turned[(zq - w) % 4][64 * zq : 64 * zq + 64], out)
            forth[chunk, w] = out
        if chunk == 0:
            pl.semaphore_wait(ready, 3)

        def send(ds, dv):
            to, w = slab_at(ds), view_at(dv)
            pltpu.make_async_remote_copy(
                src_ref=forth.at[chunk, w, pl.ds(pl.multiple_of(to * 4, 4), 4), :],
                dst_ref=seen.at[chunk, view, slab // 2, half, :],
                send_sem=p_send.at[chunk, min(dv, 1)], recv_sem=p_recv.at[chunk, dv],
                device_id=(to, tile, w), device_id_type=MESH,
            ).start()

        def start(i, _):
            ds = lax.rem(i, 16)
            for dv in (2, 1, 3):
                send(ds, dv)
            return 0

        def start_own(ds, _):
            send(ds, 0)
            return 0

        lax.fori_loop(1, 17, start, 0)
        lax.fori_loop(1, 16, start_own, 0)
        seen[chunk, view, slab // 2, half, :] = forth[
            chunk, view, pl.ds(pl.multiple_of(slab * 4, 4), 4), :
        ]

    process(0)
    exchange_m(3)
    exchange_e(3)
    process(1)
    process(2)
    process(3)

    for c in tap_copies:
        c.wait()
    for v in range(4):
        for t in range(TAPS):
            coefs[v, t] = jnp.broadcast_to(tables[v, pl.ds(t, 1), :], (8, 128))
    for z in range(16):
        quarter[z] = jnp.transpose(ext[z, HALO : 64 + HALO, :])

    first = lax.broadcasted_iota(jnp.int32, (8, 128), 0) < 4

    def accumulate(chunk, dv):
        k = ORDER[chunk]
        v = lax.rem(view + 4 - dv, 4)
        if dv:
            await_bytes(seen.at[chunk, v], p_recv.at[chunk, dv])
        else:
            await_bytes(gauge, p_recv.at[chunk, dv])
        pairs = [seen[chunk, v, j] for j in range(8)]
        swapped = [pltpu.roll(p, 4, 0) for p in pairs]
        odd = [jnp.where(first, swapped[j], swapped[j + 1]) for j in range(7)]
        odd.append(jnp.where(first, swapped[7], 0.0))
        odd.append(jnp.where(first, 0.0, swapped[0]))
        lower = final.at[k - 1] if k else edges.at[0]
        upper = final.at[k + 1] if k < 3 else edges.at[1]
        for ref, kind in ((lower, 1), (upper, -1), (final.at[k], 0)):
            for j in range(8):
                total = None
                for d in range(-RADIUS, RADIUS + 1):
                    i, parity = j + d // 2 - 8 * kind, d % 2
                    if parity:
                        if not -1 <= i <= 7:
                            continue
                        data = odd[i]
                    else:
                        if not 0 <= i <= 7:
                            continue
                        data = pairs[i]
                    term = coefs[v, RADIUS - d] * data
                    total = term if total is None else total + term
                if total is not None:
                    ref[j] = ref[j] + total

    for chunk in range(3):
        for dv in (0, 2, 1, 3):
            accumulate(chunk, dv)
    edge_down = pltpu.make_async_remote_copy(
        src_ref=edges.at[0], dst_ref=arrived.at[0],
        send_sem=edge_send.at[0], recv_sem=edge_recv.at[0],
        device_id=(slab, down, view), device_id_type=MESH,
    )
    edge_up = pltpu.make_async_remote_copy(
        src_ref=edges.at[1], dst_ref=arrived.at[1],
        send_sem=edge_send.at[1], recv_sem=edge_recv.at[1],
        device_id=(slab, up, view), device_id_type=MESH,
    )
    edge_down.start()
    edge_up.start()
    for chunk in range(4):
        await_bytes(pack_m.at[chunk, pl.ds(0, 240)], m_send.at[chunk])
        await_bytes(pack_e.at[chunk, pl.ds(0, 240)], e_send.at[chunk])
        await_bytes(gauge, p_send.at[chunk, 0])
        await_bytes(forth.at[chunk, pl.ds(0, 3)], p_send.at[chunk, 1])
    for dv in (0, 2, 1, 3):
        accumulate(3, dv)
    edge_down.wait()
    edge_up.wait()
    final[3] = final[3] + arrived[0]
    final[0] = final[0] + arrived[1]

    own_x = pl.ds(pl.multiple_of(view * 32, 32), 32)
    rows = final.reshape(256, 128)
    for z in range(4):
        turned = jnp.transpose(rows[pl.ds(z, 64, stride=4), :])
        for zq in range(4):
            at = 4 * zq + z
            out_ref[at] = quarter[at, own_x, :] * turned[32 * zq : 32 * zq + 32] * 0.25


def local(estimate, measured, psf_taps, plane_source, plane_shift):
    dma = pltpu.SemaphoreType.DMA
    smem = pl.BlockSpec(memory_space=pltpu.SMEM)
    vmem = pl.BlockSpec(memory_space=pltpu.VMEM)
    hbm = pl.BlockSpec(memory_space=pl.ANY)
    out = pl.pallas_call(
        kernel,
        name="update",
        out_shape=jax.ShapeDtypeStruct((16, 32, 64), F32),
        in_specs=[smem, smem, vmem, hbm, hbm],
        out_specs=vmem,
        scratch_shapes=[
            pltpu.VMEM((16, 96, 128), F32),
            pltpu.VMEM((16, 64, 128), F32),
            pltpu.VMEM((4, 256, 128), F32),
            pltpu.VMEM((4, 256, 128), F32),
            pltpu.VMEM((4, 256, 128), F32),
            pltpu.VMEM((4, 256, 128), F32),
            pltpu.VMEM((4, 4, 64, 128), F32),
            pltpu.VMEM((4, 4, 8, 8, 128), F32),
            pltpu.VMEM((32, 128), F32),
            pltpu.VMEM((4, 32, 128), F32),
            pltpu.VMEM((4, 32, 8, 128), F32),
            pltpu.VMEM((4, 8, 8, 128), F32),
            pltpu.VMEM((2, 8, 8, 128), F32),
            pltpu.VMEM((2, 8, 8, 128), F32),
            pltpu.VMEM((16, 128, 64), F32),
            pltpu.VMEM((128, 128), F32),
            pltpu.VMEM((384, 128), B16),
            pltpu.VMEM((256, 768), B16),
            pltpu.VMEM((256, 256), F32),
            pltpu.VMEM((256, 768), B16),
            pltpu.VMEM((256, 512), B16),
            pltpu.VMEM((384, 128), B16),
            dma((2,)), dma((2,)), dma((2,)), dma((4,)), dma((4,)),
            dma((4,)), dma((4,)), dma((4,)), dma((4,)),
            pltpu.VMEM((15, 4, 128), F32),
            dma((4, 2)), dma((4, 4)), dma((2,)), dma((2,)),
            pltpu.SemaphoreType.REGULAR,
        ],
        compiler_params=pltpu.CompilerParams(
            collective_id=0, has_side_effects=True, vmem_limit_bytes=56 * 2**20
        ),
    )(jnp.transpose(psf_taps, (1, 0, 2)), plane_shift, plane_source, estimate, measured)
    return jnp.transpose(out, (0, 2, 1))


def solution(mesh):
    in_specs = (
        P("slab", "tile", None),
        P("view", "slab", "tile", None),
        P("view", None, None),
        P("view", None),
        P("view", None),
    )
    return jax.shard_map(
        local, mesh=mesh, in_specs=in_specs, out_specs=P("slab", "tile", "view"), check_vma=False
    )
```

time: 46.9 us -> 39.3 us (0.84)
  Pallas kernels: 45.1 us -> 37.5 us
    pallas_call x1, Pallas kernels: 45.1 us -> 37.5 us  [local(): pl.pallas_call(kernel, name='update', out_shape=jax.ShapeDtypeStruct((16,...]
where the time goes in v3:
time: 39.3 us; the launch traced here: 39.2 us
  Pallas kernels  37.5 us (95%)
  local copies, waits for them, and re-layouts  1.67 us (4%)
    pallas_call x1, Pallas kernels, local(): pl.pallas_call(kernel, name='update', out_shape=jax.ShapeDtypeStruct((16,...  37.5 us
    unnamed x1, local copies, waits for them, and re-layouts  1.67 us

profile of v3, /device:TPU:1, one launch (start us, length us, event | category | flops | bytes accessed | tf_op | source)
XLA Modules:
  0.0 39.2 jit_solution(10362603442296304020)
XLA Ops:
  0.0 37.5 %update.1 = f32[16,32,64]{2,1,0:T(8,128)} custom-call(f32[3,1,31]{2,1,0:T(1,128)} %bitcast.3, s32[1,256]{1,0:T(1,128)} %shift_ref.1, s32[1,256]{1,0:T(1,128)} %source_ref.1, f32[16,64,128]{2,1,0:T(8,128)} %est_ref.1, f32[1,16,64,128]{3,2,1,0:T(8,128)} %meas_ref.1), custom_call_target="tpu_custom_call" | custom-call | tf_op jit(solution)/shard_map/update/pallas_call | solution.py:355
  37.5 1.7 %copy.7 = f32[16,64,32]{1,2,0:T(8,128)} copy(f32[16,64,32]{1,2,0:T(8,128)} %bitcast.2) | data formatting | bytes 262144

commit v4 on v3

--- a/solution.py
+++ b/solution.py
@@ -36,13 +36,14 @@
     total = taps[0]
     for t in range(1, TAPS):
         total = total + taps[t]
-    row = lax.broadcasted_iota(jnp.int32, (128, 128), 0)
-    col = lax.broadcasted_iota(jnp.int32, (128, 128), 1)
+    row = lax.broadcasted_iota(jnp.int32, (8, 128), 0)
+    col = lax.broadcasted_iota(jnp.int32, (8, 128), 1)
     off = lax.rem(col - row + RADIUS + 128, 128)
-    out = jnp.zeros((128, 128), F32)
+    top = jnp.zeros((8, 128), F32)
     for t in range(TAPS):
-        out = jnp.where(off == t, taps[TAPS - 1 - t if flip else t], out)
-    return out / jnp.full((128, 128), total)
+        top = jnp.where(off == t, taps[TAPS - 1 - t if flip else t], top)
+    top = top / jnp.full((8, 128), total)
+    return jnp.concatenate([top] + [pltpu.roll(top, 8 * b, 1) for b in range(1, 16)], axis=0)
 
 
 def wide(block):
@@ -57,14 +58,17 @@
 
 
 ORDER = (1, 0, 3, 2)
+M_SLOT = (0, 2, 3, 6)
+E_SLOT = (1, 4, 5, 7)
+RUNS = ((0, 2), (2, 4), (4, 5), (5, 6), (6, 8))
 FAR_FIRST = (10, 6, 14, 9, 11, 2, 8, 5, 7, 13, 15, 1, 3, 4, 12)
 
 
 def kernel(
-    taps_ref, shift_ref, source_ref, est_ref, meas_ref, out_ref,
-    ext, meas, pack_m, pack_e, got_m, got_e, forth, seen, table, tables, coefs,
+    taps_hbm, shift_hbm, source_hbm, est_ref, meas_ref, out_ref,
+    taps_ref, shift_ref, source_ref, ext, meas, pack, got, forth, seen, table, tables, coefs,
     final, edges, arrived, quarter, band_y, mix_x, band_z, natural, back_z, pick, back_x,
-    local_sem, halo_send, halo_recv, tap_send, tap_recv, m_send, m_recv, e_send, e_recv,
+    local_sem, halo_send, halo_recv, tap_send, tap_recv, x_send, x_recv,
     gauge, p_send, p_recv, edge_send, edge_recv, ready,
 ):
     slab, tile, view = lax.axis_index("slab"), lax.axis_index("tile"), lax.axis_index("view")
@@ -72,17 +76,15 @@
     sy, sx = slab // side, lax.rem(slab, side)
     up, down = lax.rem(tile + 1, 4), lax.rem(tile + 3, 4)
 
+    ys = [lax.rem(sy + d, side) * side for d in range(side)]
+    xs = [lax.rem(sx + d, side) for d in range(side)]
+    views = [lax.rem(view + d, 4) for d in range(4)]
+
     def slab_at(d):
-        dy, dx = d // side, lax.rem(d, side)
-        return lax.rem(sy + dy, side) * side + lax.rem(sx + dx, side)
+        return ys[d // side] + xs[d % side]
 
     def view_at(d):
-        return lax.rem(view + d, 4)
-
-    own_est = pltpu.make_async_copy(est_ref, ext.at[:, pl.ds(HALO, 64), :], local_sem.at[0])
-    own_meas = pltpu.make_async_copy(meas_ref.at[0], meas, local_sem.at[1])
-    own_est.start()
-    own_meas.start()
+        return views[d]
 
     barrier = pltpu.get_barrier_semaphore()
     pl.semaphore_signal(barrier, inc=1, device_id=(slab, tile, view_at(2)), device_id_type=MESH)
@@ -97,6 +99,15 @@
     for t in (up, down):
         pl.semaphore_signal(barrier, inc=1, device_id=(slab, t, view), device_id_type=MESH)
 
+    own_est = pltpu.make_async_copy(est_ref, ext.at[:, pl.ds(HALO, 64), :], local_sem.at[0])
+    own_meas = pltpu.make_async_copy(meas_ref.at[0], meas, local_sem.at[1])
+    own_taps = pltpu.make_async_copy(taps_hbm, taps_ref, local_sem.at[2])
+    own_shift = pltpu.make_async_copy(shift_hbm, shift_ref, local_sem.at[3])
+    own_source = pltpu.make_async_copy(source_hbm, source_ref, local_sem.at[4])
+    for c in (own_taps, own_shift, own_meas, own_est, own_source):
+        c.start()
+
+    own_taps.wait()
     taps_z = [taps_ref[0, 0, t] for t in range(TAPS)]
     taps_y = [taps_ref[1, 0, t] for t in range(TAPS)]
     taps_x = [taps_ref[2, 0, t] for t in range(TAPS)]
@@ -112,12 +123,13 @@
     band_y[...] = circulant(taps_y, False)
     mix_x[...] = right3(circulant(taps_x, True))
 
+    own_shift.wait()
     own_meas.wait()
     for j in range(16):
         amount = lax.rem(128 - shift_ref[0, slab * 16 + j], 128)
         plane = pltpu.roll(meas[j], amount, 1)
         for chunk, k in enumerate(ORDER):
-            pack_m[chunk, pl.ds(j, 16, stride=16), :] = plane[16 * k : 16 * k + 16]
+            pack[M_SLOT[chunk], pl.ds(j, 16, stride=16), :] = plane[16 * k : 16 * k + 16]
 
     def blur_rows(chunks, band, flat):
         by_y = dot(left3(band), right3(flat))
@@ -126,7 +138,7 @@
         for z in range(16):
             for i, chunk in enumerate(chunks):
                 at = 32 * z + 16 * i
-                pack_e[chunk, pl.ds(z, 16, stride=16), :] = by_x[at : at + 16, :]
+                pack[E_SLOT[chunk], pl.ds(z, 16, stride=16), :] = by_x[at : at + 16, :]
 
     own_est.wait()
     blur_rows(
@@ -152,31 +164,27 @@
 
     mine = pl.ds(pl.multiple_of(slab * 16, 16), 16)
 
-    def exchange(chunk, pack, got, send, recv):
-        def start(d, _):
+    def exchange(run):
+        lo, hi = RUNS[run]
+        for d in FAR_FIRST:
             to = slab_at(d)
             pltpu.make_async_remote_copy(
-                src_ref=pack.at[chunk, pl.ds(pl.multiple_of(to * 16, 16), 16), :],
-                dst_ref=got.at[chunk, mine, :],
-                send_sem=send.at[chunk], recv_sem=recv.at[chunk],
+                src_ref=pack.at[lo:hi, pl.ds(pl.multiple_of(to * 16, 16), 16), :],
+                dst_ref=got.at[lo:hi, mine, :],
+                send_sem=x_send.at[run], recv_sem=x_recv.at[run],
                 device_id=(to, tile, view), device_id_type=MESH,
             ).start()
-            return 0
-
-        lax.fori_loop(1, 16, start, 0)
-        got[chunk, mine, :] = pack[chunk, mine, :]
+        for slot in range(lo, hi):
+            got[slot, mine, :] = pack[slot, mine, :]
 
     def await_bytes(ref, sem):
         pltpu.make_async_copy(ref, ref, sem).wait()
 
-    def exchange_m(chunk):
-        exchange(chunk, pack_m, got_m, m_send, m_recv)
-
-    def exchange_e(chunk):
-        exchange(chunk, pack_e, got_e, e_send, e_recv)
-
-    exchange_m(0)
-    exchange_e(0)
+    def await_run(run):
+        lo, hi = RUNS[run]
+        await_bytes(got.at[lo:hi, pl.ds(0, 240)], x_recv.at[run])
+
+    exchange(0)
     tap_copies = []
     for d in (2, 1, 3):
         c = pltpu.make_async_remote_copy(
@@ -189,16 +197,15 @@
         pl.semaphore_signal(
             ready, inc=1, device_id=(slab, tile, view_at(d)), device_id_type=MESH
         )
-    exchange_m(1)
-    exchange_m(2)
+    exchange(1)
 
     band_z[...] = left3(wide(circulant(taps_z, False)))
-    natural[...] = wide(circulant(taps_z, True))
+    both = wide(circulant(taps_z, True))
+    natural[0], natural[1] = both[:, 0:128], both[:, 128:256]
     for zq in range(4):
-        rows = jnp.concatenate(
-            [natural[16 * s + 4 * zq : 16 * s + 4 * zq + 4, :] for s in range(16)], axis=0
-        )
-        back_z[64 * zq : 64 * zq + 64, :] = left3(rows)
+        rows = [natural[i, pl.ds(zq, 64, stride=4), :] for i in range(2)]
+        back_z[64 * zq : 64 * zq + 64, :] = left3(jnp.concatenate(rows, axis=1))
+    own_source.wait()
     plane_of = lax.broadcasted_iota(jnp.int32, (256, 256), 0)
     shown = jnp.where(jnp.broadcast_to(source_ref[...], (256, 256)) == plane_of, 1.0, 0.0)
     shown = shown.astype(B16)
@@ -214,18 +221,18 @@
         jnp.concatenate([band_y[16:32, 0:96], band_y[64:80, 0:96]], axis=0),
         jnp.concatenate([ext[z] for z in range(16)], axis=1),
     )
-    exchange_e(1)
-    exchange_e(2)
+    exchange(2)
+    exchange(3)
 
     block = lax.broadcasted_iota(jnp.int32, (64, 128), 1) // 32
     half = pl.ds(pl.multiple_of(lax.rem(slab, 2) * 4, 4), 4)
 
     def process(chunk):
-        await_bytes(got_m.at[chunk, pl.ds(0, 240)], m_recv.at[chunk])
-        m_high, m_low = split(got_m[chunk])
+        for run in ((0,), (1, 2), (3,), (4,))[chunk]:
+            await_run(run)
+        m_high, m_low = split(got[M_SLOT[chunk]])
         routed = dot(pick[...], jnp.concatenate([m_high, m_low], axis=0))
-        await_bytes(got_e.at[chunk, pl.ds(0, 240)], e_recv.at[chunk])
-        blurred = dot(band_z[...], right3(got_e[chunk]))
+        blurred = dot(band_z[...], right3(got[E_SLOT[chunk]]))
         pulled = dot(back_z[...], right3(routed / blurred))
         by_x = dot(left3(pulled), back_x[...])
         turned = [by_x] + [pltpu.roll(by_x, 32 * m, 1) for m in (1, 2, 3)]
@@ -246,25 +253,17 @@
                 device_id=(to, tile, w), device_id_type=MESH,
             ).start()
 
-        def start(i, _):
-            ds = lax.rem(i, 16)
-            for dv in (2, 1, 3):
+        for ds in FAR_FIRST:
+            for dv in (2, 1, 3, 0):
                 send(ds, dv)
-            return 0
-
-        def start_own(ds, _):
-            send(ds, 0)
-            return 0
-
-        lax.fori_loop(1, 17, start, 0)
-        lax.fori_loop(1, 16, start_own, 0)
+        for dv in (2, 1, 3):
+            send(0, dv)
         seen[chunk, view, slab // 2, half, :] = forth[
             chunk, view, pl.ds(pl.multiple_of(slab * 4, 4), 4), :
         ]
 
     process(0)
-    exchange_m(3)
-    exchange_e(3)
+    exchange(4)
     process(1)
     process(2)
     process(3)
@@ -327,10 +326,10 @@
     edge_down.start()
     edge_up.start()
     for chunk in range(4):
-        await_bytes(pack_m.at[chunk, pl.ds(0, 240)], m_send.at[chunk])
-        await_bytes(pack_e.at[chunk, pl.ds(0, 240)], e_send.at[chunk])
         await_bytes(gauge, p_send.at[chunk, 0])
         await_bytes(forth.at[chunk, pl.ds(0, 3)], p_send.at[chunk, 1])
+    for run, (lo, hi) in enumerate(RUNS):
+        await_bytes(pack.at[lo:hi, pl.ds(0, 240)], x_send.at[run])
     for dv in (0, 2, 1, 3):
         accumulate(3, dv)
     edge_down.wait()
@@ -343,28 +342,28 @@
     for z in range(4):
         turned = jnp.transpose(rows[pl.ds(z, 64, stride=4), :])
         for zq in range(4):
-            at = 4 * zq + z
+            at = 4 * z + zq
             out_ref[at] = quarter[at, own_x, :] * turned[32 * zq : 32 * zq + 32] * 0.25
 
 
 def local(estimate, measured, psf_taps, plane_source, plane_shift):
     dma = pltpu.SemaphoreType.DMA
-    smem = pl.BlockSpec(memory_space=pltpu.SMEM)
     vmem = pl.BlockSpec(memory_space=pltpu.VMEM)
     hbm = pl.BlockSpec(memory_space=pl.ANY)
     out = pl.pallas_call(
         kernel,
         name="update",
-        out_shape=jax.ShapeDtypeStruct((16, 32, 64), F32),
-        in_specs=[smem, smem, vmem, hbm, hbm],
+        out_shape=pltpu.VMEM((16, 32, 64), F32),
+        in_specs=[hbm] * 5,
         out_specs=vmem,
         scratch_shapes=[
+            pltpu.SMEM((3, 1, TAPS), F32),
+            pltpu.SMEM((1, 256), jnp.int32),
+            pltpu.VMEM((1, 256), jnp.int32),
             pltpu.VMEM((16, 96, 128), F32),
             pltpu.VMEM((16, 64, 128), F32),
-            pltpu.VMEM((4, 256, 128), F32),
-            pltpu.VMEM((4, 256, 128), F32),
-            pltpu.VMEM((4, 256, 128), F32),
-            pltpu.VMEM((4, 256, 128), F32),
+            pltpu.VMEM((8, 256, 128), F32),
+            pltpu.VMEM((8, 256, 128), F32),
             pltpu.VMEM((4, 4, 64, 128), F32),
             pltpu.VMEM((4, 4, 8, 8, 128), F32),
             pltpu.VMEM((32, 128), F32),
@@ -377,12 +376,12 @@
             pltpu.VMEM((128, 128), F32),
             pltpu.VMEM((384, 128), B16),
             pltpu.VMEM((256, 768), B16),
-            pltpu.VMEM((256, 256), F32),
+            pltpu.VMEM((2, 256, 128), F32),
             pltpu.VMEM((256, 768), B16),
             pltpu.VMEM((256, 512), B16),
             pltpu.VMEM((384, 128), B16),
-            dma((2,)), dma((2,)), dma((2,)), dma((4,)), dma((4,)),
-            dma((4,)), dma((4,)), dma((4,)), dma((4,)),
+            dma((5,)), dma((2,)), dma((2,)), dma((4,)), dma((4,)),
+            dma((5,)), dma((5,)),
             pltpu.VMEM((15, 4, 128), F32),
             dma((4, 2)), dma((4, 4)), dma((2,)), dma((2,)),
             pltpu.SemaphoreType.REGULAR,

time: 39.3 us -> 36.9 us (0.939)
  Pallas kernels: 37.5 us -> 36.1 us
  local copies, waits for them, and re-layouts: 1.67 us -> 0.71 us
    pallas_call x1, Pallas kernels: 37.5 us -> 36.1 us  [local(): pl.pallas_call(kernel, name='update', out_shape=pltpu.VMEM((16, 32, 64),...]
    unnamed x1, local copies, waits for them, and re-layouts: 1.67 us -> 0.71 us
where the time goes in v4:
time: 36.9 us; the launch traced here: 36.8 us
  Pallas kernels  36.1 us (98%)
  local copies, waits for them, and re-layouts  0.71 us (2%)
    pallas_call x1, Pallas kernels, local(): pl.pallas_call(kernel, name='update', out_shape=pltpu.VMEM((16, 32, 64),...  36.1 us

profile of v4, /device:TPU:1, one launch (start us, length us, event | category | flops | bytes accessed | tf_op | source)
XLA Modules:
  0.0 36.8 jit_solution(5001677565684172886)
XLA Ops:
  0.0 36.1 %update.1 = f32[16,32,64]{2,1,0:T(8,128)S(1)} custom-call(f32[3,1,31]{2,1,0:T(1,128)} %bitcast.3, s32[1,256]{1,0:T(1,128)} %shift_hbm.1, s32[1,256]{1,0:T(1,128)} %source_hbm.1, f32[16,64,128]{2,1,0:T(8,128)} %est_ref.1, f32[1,16,64,128]{3,2,1,0:T(8,128)} %meas_ref.1), custom_call_target="tpu_custom_call" | custom-call | tf_op jit(solution)/shard_map/update/pallas_call | solution.py:353
  36.1 0.7 %copy.7 = f32[16,64,32]{1,2,0:T(8,128)} copy(f32[16,64,32]{1,2,0:T(8,128)S(1)} %bitcast.2) | data formatting | bytes 262144

commit v5 on v4

--- a/solution.py
+++ b/solution.py
@@ -166,14 +166,24 @@
 
     def exchange(run):
         lo, hi = RUNS[run]
-        for d in FAR_FIRST:
-            to = slab_at(d)
+
+        def send(to):
             pltpu.make_async_remote_copy(
                 src_ref=pack.at[lo:hi, pl.ds(pl.multiple_of(to * 16, 16), 16), :],
                 dst_ref=got.at[lo:hi, mine, :],
                 send_sem=x_send.at[run], recv_sem=x_recv.at[run],
                 device_id=(to, tile, view), device_id_type=MESH,
             ).start()
+
+        def start(dy, _):
+            row = lax.rem(sy + dy, side) * side
+            for dx in (2, 1, 3, 0):
+                send(row + xs[dx])
+            return 0
+
+        lax.fori_loop(1, side, start, 0)
+        for dx in (2, 1, 3):
+            send(ys[0] + xs[dx])
         for slot in range(lo, hi):
             got[slot, mine, :] = pack[slot, mine, :]
 
@@ -241,33 +251,49 @@
             for zq in (2, 1, 0):
                 out = jnp.where(block == zq, turned[(zq - w) % 4][64 * zq : 64 * zq + 64], out)
             forth[chunk, w] = out
-        if chunk == 0:
-            pl.semaphore_wait(ready, 3)
-
-        def send(ds, dv):
-            to, w = slab_at(ds), view_at(dv)
+        seen[chunk, view, slab // 2, half, :] = forth[
+            chunk, view, pl.ds(pl.multiple_of(slab * 4, 4), 4), :
+        ]
+
+    def send_quarter(chunk, w):
+        dv = lax.rem(w - view + 4, 4)
+
+        def send(to, sem):
             pltpu.make_async_remote_copy(
                 src_ref=forth.at[chunk, w, pl.ds(pl.multiple_of(to * 4, 4), 4), :],
                 dst_ref=seen.at[chunk, view, slab // 2, half, :],
-                send_sem=p_send.at[chunk, min(dv, 1)], recv_sem=p_recv.at[chunk, dv],
+                send_sem=p_send.at[chunk, sem], recv_sem=p_recv.at[chunk, dv],
                 device_id=(to, tile, w), device_id_type=MESH,
             ).start()
 
-        for ds in FAR_FIRST:
-            for dv in (2, 1, 3, 0):
-                send(ds, dv)
-        for dv in (2, 1, 3):
-            send(0, dv)
-        seen[chunk, view, slab // 2, half, :] = forth[
-            chunk, view, pl.ds(pl.multiple_of(slab * 4, 4), 4), :
-        ]
+        def start(dy, _):
+            row = lax.rem(sy + dy, side) * side
+            for dx in (2, 1, 3, 0):
+                send(row + xs[dx], 0)
+            return 0
+
+        lax.fori_loop(1, side, start, 0)
+        for dx in (2, 1, 3):
+            send(ys[0] + xs[dx], 0)
+
+        @pl.when(w != view)
+        def _():
+            send(slab, 1)
 
     process(0)
+    pl.semaphore_wait(ready, 3)
+    for w in (0, 1, 2, 3):
+        send_quarter(0, w)
     exchange(4)
     process(1)
+    for w in (0, 1, 2, 3):
+        send_quarter(1, w)
     process(2)
+    for w in (0, 1, 2, 3):
+        send_quarter(2, w)
     process(3)
-
+    for w in (0, 1, 2, 3):
+        send_quarter(3, w)
     for c in tap_copies:
         c.wait()
     for v in range(4):
@@ -325,11 +351,6 @@
     )
     edge_down.start()
     edge_up.start()
-    for chunk in range(4):
-        await_bytes(gauge, p_send.at[chunk, 0])
-        await_bytes(forth.at[chunk, pl.ds(0, 3)], p_send.at[chunk, 1])
-    for run, (lo, hi) in enumerate(RUNS):
-        await_bytes(pack.at[lo:hi, pl.ds(0, 240)], x_send.at[run])
     for dv in (0, 2, 1, 3):
         accumulate(3, dv)
     edge_down.wait()
@@ -344,6 +365,11 @@
         for zq in range(4):
             at = 4 * z + zq
             out_ref[at] = quarter[at, own_x, :] * turned[32 * zq : 32 * zq + 32] * 0.25
+    for chunk in range(4):
+        await_bytes(got.at[0, pl.ds(0, 240)], p_send.at[chunk, 0])
+        await_bytes(gauge.at[pl.ds(0, 3)], p_send.at[chunk, 1])
+    for run, (lo, hi) in enumerate(RUNS):
+        await_bytes(pack.at[lo:hi, pl.ds(0, 240)], x_send.at[run])
 
 
 def local(estimate, measured, psf_taps, plane_source, plane_shift):

time: 36.9 us -> 36.8 us (level)
  no operation moved by 1% of the time
where the time goes in v5:
time: 36.8 us
  Pallas kernels  36 us (98%)
  local copies, waits for them, and re-layouts  0.71 us (2%)
    pallas_call x1, Pallas kernels, local(): pl.pallas_call(kernel, name='update', out_shape=pltpu.VMEM((16, 32, 64),...  36 us

profile of v5, /device:TPU:1, one launch (start us, length us, event | category | flops | bytes accessed | tf_op | source)
XLA Modules:
  0.0 36.8 jit_solution(12012246711231842369)
XLA Ops:
  0.0 36.0 %update.1 = f32[16,32,64]{2,1,0:T(8,128)S(1)} custom-call(f32[3,1,31]{2,1,0:T(1,128)} %bitcast.3, s32[1,256]{1,0:T(1,128)} %shift_hbm.1, s32[1,256]{1,0:T(1,128)} %source_hbm.1, f32[16,64,128]{2,1,0:T(8,128)} %est_ref.1, f32[1,16,64,128]{3,2,1,0:T(8,128)} %meas_ref.1), custom_call_target="tpu_custom_call" | custom-call | tf_op jit(solution)/shard_map/update/pallas_call | solution.py:379
  36.1 0.7 %copy.7 = f32[16,64,32]{1,2,0:T(8,128)} copy(f32[16,64,32]{1,2,0:T(8,128)S(1)} %bitcast.2) | data formatting | bytes 262144

commit v6 on v5

--- a/solution.py
+++ b/solution.py
@@ -255,8 +255,8 @@
             chunk, view, pl.ds(pl.multiple_of(slab * 4, 4), 4), :
         ]
 
-    def send_quarter(chunk, w):
-        dv = lax.rem(w - view + 4, 4)
+    def send_quarter(chunk, dv):
+        w = view_at(dv)
 
         def send(to, sem):
             pltpu.make_async_remote_copy(
@@ -266,34 +266,33 @@
                 device_id=(to, tile, w), device_id_type=MESH,
             ).start()
 
-        def start(dy, _):
-            row = lax.rem(sy + dy, side) * side
+        def start(i, _):
+            row = lax.rem(sy + lax.rem(4 - i, 3) + 1, side) * side
             for dx in (2, 1, 3, 0):
                 send(row + xs[dx], 0)
             return 0
 
-        lax.fori_loop(1, side, start, 0)
+        lax.fori_loop(0, 3, start, 0)
         for dx in (2, 1, 3):
             send(ys[0] + xs[dx], 0)
-
-        @pl.when(w != view)
-        def _():
+        if dv:
             send(slab, 1)
 
     process(0)
     pl.semaphore_wait(ready, 3)
-    for w in (0, 1, 2, 3):
-        send_quarter(0, w)
+    for dv in (2, 1, 3, 0):
+        send_quarter(0, dv)
     exchange(4)
     process(1)
-    for w in (0, 1, 2, 3):
-        send_quarter(1, w)
+    for dv in (2, 1, 3, 0):
+        send_quarter(1, dv)
     process(2)
-    for w in (0, 1, 2, 3):
-        send_quarter(2, w)
+    for dv in (2, 1, 3, 0):
+        send_quarter(2, dv)
     process(3)
-    for w in (0, 1, 2, 3):
-        send_quarter(3, w)
+    for dv in (2, 1, 3, 0):
+        send_quarter(3, dv)
+
     for c in tap_copies:
         c.wait()
     for v in range(4):

time: 36.8 us -> 36.9 us (level)
  no operation moved by 1% of the time
where the time goes in v6:
time: 36.9 us; the launch traced here: 36.8 us
  Pallas kernels  36.1 us (98%)
  local copies, waits for them, and re-layouts  0.71 us (2%)
    pallas_call x1, Pallas kernels, local(): pl.pallas_call(kernel, name='update', out_shape=pltpu.VMEM((16, 32, 64),...  36.1 us

profile of v6, /device:TPU:1, one launch (start us, length us, event | category | flops | bytes accessed | tf_op | source)
XLA Modules:
  0.0 36.8 jit_solution(15411853604023425386)
XLA Ops:
  0.0 36.1 %update.1 = f32[16,32,64]{2,1,0:T(8,128)S(1)} custom-call(f32[3,1,31]{2,1,0:T(1,128)} %bitcast.3, s32[1,256]{1,0:T(1,128)} %shift_hbm.1, s32[1,256]{1,0:T(1,128)} %source_hbm.1, f32[16,64,128]{2,1,0:T(8,128)} %est_ref.1, f32[1,16,64,128]{3,2,1,0:T(8,128)} %meas_ref.1), custom_call_target="tpu_custom_call" | custom-call | tf_op jit(solution)/shard_map/update/pallas_call | solution.py:378
  36.1 0.7 %copy.7 = f32[16,64,32]{1,2,0:T(8,128)} copy(f32[16,64,32]{1,2,0:T(8,128)S(1)} %bitcast.2) | data formatting | bytes 262144
